TPU v7x, 32 devices: a whole 2x2x4 slice. The times are simulated.
32 devices in a mesh: dp: 8 (over z, y), section: 4 (over x, core).
Axes of the slice: x: 2, y: 2, z: 4, core: 2. Of those that a mesh axis runs over, the one named last changes fastest.
Arguments:
- vis_embed: bfloat16 [12288, 768], P(('dp', 'section')), may hold values from -6 to 6
- latent_cot: bfloat16 [12288, 768], P(('dp', 'section')), may hold values from -6 to 6
- reg_queries: bfloat16 [12288, 768], P(('dp', 'section')), may hold values from -6 to 6
- out_cot: bfloat16 [12288, 768], P(('dp', 'section')), may hold values from -6 to 6
- section_matrix: bfloat16 [4, 768, 3072], P('section')
- down_weight: bfloat16 [6144, 768], P('section'), may hold values from -0.109375 to 0.109375
- enc_vectors: float32 [6, 768], replicated, as said below
- reg_vectors: float32 [10, 768], replicated, as said below
- mlp_vectors: float32 [2, 4, 768], replicated, as said below
- hidden_bias: float32 [2, 3072], replicated, may hold values from -1.5 to 1.5
- pos_table: float32 [256, 768], replicated, may hold values from -6 to 6
- image_lengths: int32 [32, 4], P('dp'), may hold values from 1 to 128, as said below
- vis_index: int32 [12288], P('dp'), may hold values from 0 to 255, as said below
- mask_index: int32 [12288], P('dp'), may hold values from 0 to 255, as said below
Outputs:
- latents: bfloat16 [12288, 768], P(('dp', 'section'))
- regressed: bfloat16 [12288, 768], P(('dp', 'section'))
- vis_grad: bfloat16 [12288, 768], P(('dp', 'section'))
- query_grad: bfloat16 [12288, 768], P(('dp', 'section'))
- grad_section_matrix: float32 [4, 768, 3072], P('section')
- grad_down: float32 [6144, 768], P('section')
- grad_enc_vectors: float32 [6, 768], replicated
- grad_reg_vectors: float32 [10, 768], replicated
- grad_mlp_vectors: float32 [2, 4, 768], replicated
- grad_hidden_bias: float32 [2, 3072], replicated
Inputs may be any that keep to these rules, and one draw needn't show every extreme that they name: `image_lengths`: each row sums to 384, and its largest entry is 128. `vis_index`: for an image with n visible patches, its n visible places and the n masked places at the same rows are 0 to 2 n - 1, each once. `mask_index`: see vis_index. `enc_vectors`: gain and layer-scale rows are positive. `reg_vectors`: gain and layer-scale rows are positive. `mlp_vectors`: gain and layer-scale rows are positive.
All inputs are finite; a program needn't handle non-finite values.
Results may differ from a plain program's by a relative error of at most 0.015.
Values may be sent and summed in bfloat16 or wider, within the bound.
A program may use at most 192 MiB of HBM per device.

v0:
```python
import math

import jax
import jax.numpy as jnp
from jax import lax
from jax.sharding import PartitionSpec as P

H = 12
CAP = 384
MB = 4


epsilon = 1e-06
masked_score = -1e30
half_root = 1.0 / math.sqrt(2.0)
density_scale = 1.0 / math.sqrt(2.0 * math.pi)


def shifted(block, axis, distance):
    devices = range(lax.axis_size(axis))
    route = [(i - distance, i) for i in devices if i - distance in devices]
    return lax.ppermute(block, axis, route)


def shortened(x):
    return jax.tree.map(lambda a: a.astype(jnp.bfloat16) if a.dtype == jnp.float32 else a, x)


def project(left_side, right_side):
    return jnp.dot(left_side, right_side, preferred_element_type=jnp.float32)


def project_back(left_side, right_side):
    return lax.dot_general(
        left_side, right_side, (((1,), (1,)), ((), ())), preferred_element_type=jnp.float32
    )


def outer_sum(left_side, right_side):
    return lax.dot_general(
        left_side, right_side, (((0,), (0,)), ((), ())), preferred_element_type=jnp.float32
    )


def column_total(values):
    return jnp.sum(values.astype(jnp.float32), axis=0)


def layer_norm(values, gain_rows, offsets):
    average = jnp.mean(values, axis=-1, keepdims=True)
    centred = values - average
    spread = jnp.mean(centred * centred, axis=-1, keepdims=True)
    inverse = lax.rsqrt(spread + epsilon)
    normed = centred * inverse
    return (normed * gain_rows + offsets, (normed, inverse))


def layer_norm_back(gradient, gain_rows, stored):
    normed, inverse = stored
    scaled = gradient * gain_rows
    level_term = jnp.mean(scaled, axis=-1, keepdims=True)
    slope_term = jnp.mean(scaled * normed, axis=-1, keepdims=True)
    d_values = inverse * (scaled - level_term - normed * slope_term)
    return (d_values, jnp.sum(gradient * normed, axis=0), jnp.sum(gradient, axis=0))


def attention_core(query_rows, key_rows, value_rows, allowed):
    row_count = query_rows.shape[0]
    key_number = key_rows.shape[0]
    head_width = query_rows.shape[1] // H
    heads_q = query_rows.reshape(row_count, H, head_width)
    heads_k = key_rows.reshape(key_number, H, head_width)
    heads_v = value_rows.reshape(key_number, H, head_width)
    scores = jnp.einsum(
        "qhd,khd->hqk", heads_q, heads_k, preferred_element_type=jnp.float32
    ) * head_width ** (-0.5)
    scores = jnp.where(allowed[None], scores, masked_score)
    highest = jnp.max(scores, axis=-1, keepdims=True)
    raised = jnp.exp(scores - highest)
    prob_rows = raised / jnp.sum(raised, axis=-1, keepdims=True)
    mixed_heads = jnp.einsum(
        "hqk,khd->qhd", prob_rows.astype(jnp.bfloat16), heads_v, preferred_element_type=jnp.float32
    )
    return (mixed_heads.reshape(row_count, H * head_width).astype(jnp.bfloat16), prob_rows)


def attention_core_back(d_mixed, query_rows, key_rows, value_rows, prob_rows):
    row_count = query_rows.shape[0]
    key_number = key_rows.shape[0]
    head_width = query_rows.shape[1] // H
    model_width = H * head_width
    heads_q = query_rows.reshape(row_count, H, head_width)
    heads_k = key_rows.reshape(key_number, H, head_width)
    heads_v = value_rows.reshape(key_number, H, head_width)
    heads_d = d_mixed.reshape(row_count, H, head_width)
    d_probs = jnp.einsum("qhd,khd->hqk", heads_d, heads_v, preferred_element_type=jnp.float32)
    centre_term = jnp.sum(prob_rows * d_probs, axis=-1, keepdims=True)
    d_scores = (prob_rows * (d_probs - centre_term)).astype(jnp.bfloat16)
    scale_factor = head_width ** (-0.5)
    d_query = (
        jnp.einsum("hqk,khd->qhd", d_scores, heads_k, preferred_element_type=jnp.float32)
        * scale_factor
    )
    d_key = (
        jnp.einsum("hqk,qhd->khd", d_scores, heads_q, preferred_element_type=jnp.float32)
        * scale_factor
    )
    d_value = jnp.einsum(
        "hqk,qhd->khd", prob_rows.astype(jnp.bfloat16), heads_d, preferred_element_type=jnp.float32
    )
    return (
        d_query.reshape(row_count, model_width).astype(jnp.bfloat16),
        d_key.reshape(key_number, model_width).astype(jnp.bfloat16),
        d_value.reshape(key_number, model_width).astype(jnp.bfloat16),
    )


def encoder_attention(residual, matrix, vectors, allowed):
    model_width = residual.shape[1]
    normed, stored = layer_norm(residual, vectors[0], vectors[1])
    normed_low = normed.astype(jnp.bfloat16)
    packed = project(normed_low, matrix[:, : 3 * model_width])
    query_rows = (packed[:, :model_width] + vectors[2]).astype(jnp.bfloat16)
    key_rows = packed[:, model_width : 2 * model_width].astype(jnp.bfloat16)
    value_rows = (packed[:, 2 * model_width :] + vectors[3]).astype(jnp.bfloat16)
    mixed_heads, prob_rows = attention_core(query_rows, key_rows, value_rows, allowed)
    branch = project_back(mixed_heads, matrix[:, 3 * model_width :]) + vectors[4]
    outcome = residual + vectors[5] * branch
    return (
        outcome,
        (stored, normed_low, query_rows, key_rows, value_rows, mixed_heads, prob_rows, branch),
    )


def encoder_attention_back(gradient, residual, matrix, vectors, allowed):
    model_width = residual.shape[1]
    outcome, kept_values = encoder_attention(residual, matrix, vectors, allowed)
    stored, normed_low, query_rows, key_rows, value_rows, mixed_heads, prob_rows, branch = (
        kept_values
    )
    d_branch = (gradient * vectors[5]).astype(jnp.bfloat16)
    d_mixed = project(d_branch, matrix[:, 3 * model_width :]).astype(jnp.bfloat16)
    d_query, d_key, d_value = attention_core_back(
        d_mixed, query_rows, key_rows, value_rows, prob_rows
    )
    d_packed = jnp.concatenate([d_query, d_key, d_value], axis=1)
    d_normed = project_back(d_packed, matrix[:, : 3 * model_width])
    d_residual, d_gain, d_offset = layer_norm_back(d_normed, vectors[0], stored)
    grad_matrix = jnp.concatenate(
        [outer_sum(normed_low, d_packed), outer_sum(d_branch, mixed_heads)], axis=1
    )
    grad_vectors = jnp.stack(
        [
            d_gain,
            d_offset,
            column_total(d_query),
            column_total(d_value),
            column_total(d_branch),
            jnp.sum(gradient * branch, axis=0),
        ]
    )
    return (gradient + d_residual, grad_matrix, grad_vectors)


def regressor_attention(latent_rows, queries, pos_vis, pos_mask, matrix, vectors, allowed):
    model_width = queries.shape[1]
    q_source = queries + pos_mask
    k_source = jnp.concatenate([latent_rows + pos_vis, q_source], axis=0)
    v_source = jnp.concatenate([latent_rows, queries], axis=0)
    q_normed, q_stored = layer_norm(q_source, vectors[0], vectors[1])
    k_normed, k_stored = layer_norm(k_source, vectors[2], vectors[3])
    v_normed, v_stored = layer_norm(v_source, vectors[4], vectors[5])
    q_low = q_normed.astype(jnp.bfloat16)
    k_low = k_normed.astype(jnp.bfloat16)
    v_low = v_normed.astype(jnp.bfloat16)
    query_rows = (project(q_low, matrix[:, :model_width]) + vectors[6]).astype(jnp.bfloat16)
    key_rows = project(k_low, matrix[:, model_width : 2 * model_width]).astype(jnp.bfloat16)
    value_rows = (project(v_low, matrix[:, 2 * model_width : 3 * model_width]) + vectors[7]).astype(
        jnp.bfloat16
    )
    mixed_heads, prob_rows = attention_core(query_rows, key_rows, value_rows, allowed)
    branch = project_back(mixed_heads, matrix[:, 3 * model_width :]) + vectors[8]
    outcome = queries + vectors[9] * branch
    kept_values = (
        q_stored,
        k_stored,
        v_stored,
        q_low,
        k_low,
        v_low,
        query_rows,
        key_rows,
        value_rows,
        mixed_heads,
        prob_rows,
        branch,
    )
    return (outcome, kept_values)


def regressor_attention_back(
    gradient, latent_rows, queries, pos_vis, pos_mask, matrix, vectors, allowed
):
    model_width = queries.shape[1]
    row_count = queries.shape[0]
    outcome, kept_values = regressor_attention(
        latent_rows, queries, pos_vis, pos_mask, matrix, vectors, allowed
    )
    (
        q_stored,
        k_stored,
        v_stored,
        q_low,
        k_low,
        v_low,
        query_rows,
        key_rows,
        value_rows,
        mixed_heads,
        prob_rows,
        branch,
    ) = kept_values
    d_branch = (gradient * vectors[9]).astype(jnp.bfloat16)
    d_mixed = project(d_branch, matrix[:, 3 * model_width :]).astype(jnp.bfloat16)
    d_query, d_key, d_value = attention_core_back(
        d_mixed, query_rows, key_rows, value_rows, prob_rows
    )
    dq_normed = project_back(d_query, matrix[:, :model_width])
    dk_normed = project_back(d_key, matrix[:, model_width : 2 * model_width])
    dv_normed = project_back(d_value, matrix[:, 2 * model_width : 3 * model_width])
    dq_source, q_gain, q_offset = layer_norm_back(dq_normed, vectors[0], q_stored)
    dk_source, k_gain, k_offset = layer_norm_back(dk_normed, vectors[2], k_stored)
    dv_source, v_gain, v_offset = layer_norm_back(dv_normed, vectors[4], v_stored)
    d_latent = dk_source[:row_count] + dv_source[:row_count]
    d_queries = gradient + dq_source + dk_source[row_count:] + dv_source[row_count:]
    grad_matrix = jnp.concatenate(
        [
            outer_sum(q_low, d_query),
            outer_sum(k_low, d_key),
            outer_sum(v_low, d_value),
            outer_sum(d_branch, mixed_heads),
        ],
        axis=1,
    )
    grad_vectors = jnp.stack(
        [
            q_gain,
            q_offset,
            k_gain,
            k_offset,
            v_gain,
            v_offset,
            column_total(d_query),
            column_total(d_value),
            column_total(d_branch),
            jnp.sum(gradient * branch, axis=0),
        ]
    )
    return (d_latent, d_queries, grad_matrix, grad_vectors)


def feed_forward(residual, up_matrix, down_matrix, vectors, hidden_offset):
    normed, stored = layer_norm(residual, vectors[0], vectors[1])
    normed_low = normed.astype(jnp.bfloat16)
    hidden = project(normed_low, up_matrix) + hidden_offset
    active = jax.nn.gelu(hidden, approximate=False).astype(jnp.bfloat16)
    branch = project(active, down_matrix) + vectors[2]
    outcome = residual + vectors[3] * branch
    return (outcome, (stored, normed_low, hidden, active, branch))


def feed_forward_back(gradient, residual, up_matrix, down_matrix, vectors, hidden_offset):
    outcome, kept_values = feed_forward(residual, up_matrix, down_matrix, vectors, hidden_offset)
    stored, normed_low, hidden, active, branch = kept_values
    d_branch = (gradient * vectors[3]).astype(jnp.bfloat16)
    d_active = project_back(d_branch, down_matrix)
    slope_rows = (
        0.5 * (1.0 + lax.erf(hidden * half_root))
        + hidden * jnp.exp(-0.5 * hidden * hidden) * density_scale
    )
    d_hidden = (d_active * slope_rows).astype(jnp.bfloat16)
    d_normed = project_back(d_hidden, up_matrix)
    d_residual, d_gain, d_offset = layer_norm_back(d_normed, vectors[0], stored)
    grad_up = outer_sum(normed_low, d_hidden)
    grad_down = outer_sum(active, d_branch)
    grad_vectors = jnp.stack(
        [d_gain, d_offset, column_total(d_branch), jnp.sum(gradient * branch, axis=0)]
    )
    return (gradient + d_residual, grad_up, grad_down, grad_vectors, column_total(d_hidden))


def lookup(pos_rows, indices):
    onehot = (indices[:, None] == jnp.arange(pos_rows.shape[0])[None, :]).astype(jnp.float32)
    return jnp.dot(onehot, pos_rows, precision=lax.Precision.HIGHEST)


def image_mask(image_row):
    return image_row[:, None] == image_row[None, :]


def image_keys(image_row):
    return image_row[:, None] == jnp.concatenate([image_row, image_row])[None, :]


def pick_row(array, index):
    return lax.dynamic_index_in_dim(array, index, 0, keepdims=False)


def put_row(array, row_value, index):
    return lax.dynamic_update_index_in_dim(array, row_value, index, 0)


def settle(first_part, down_part, section_index):
    half_rows = down_part.shape[0] // 2
    returned = shifted(down_part[:half_rows].astype(jnp.bfloat16), "section", -1).astype(
        jnp.float32
    )
    own_half = jnp.where(section_index % 2 == 1, down_part[half_rows:], returned)
    return (first_part, own_half)


def add_grads(grad_parts, first_part, down_part):
    return (grad_parts[0] + first_part, grad_parts[1] + down_part)


def body(
    vis_embed,
    latent_cot,
    reg_queries,
    out_cot,
    section_matrix,
    down_weight,
    enc_vectors,
    reg_vectors,
    mlp_vectors,
    hidden_bias,
    pos_table,
    image_lengths,
    vis_index,
    mask_index,
):
    model_width = vis_embed.shape[1]
    section_count = lax.axis_size("section")
    section_index = lax.axis_index("section")
    odd_section = section_index % 2 == 1
    matrix = section_matrix[0]
    hidden_width = matrix.shape[1]
    stacked = jnp.stack([vis_embed, latent_cot, reg_queries, out_cot])
    section_feed = lax.all_to_all(
        stacked, "section", split_axis=0, concat_axis=1, tiled=True
    ).reshape(MB, CAP, model_width)
    fetched = shifted(down_weight, "section", 1)
    full_down = jnp.concatenate([fetched, down_weight], axis=0)
    image_ends = jnp.cumsum(image_lengths, axis=1)
    images = jnp.sum(jnp.arange(CAP)[None, :, None] >= image_ends[:, None, :], axis=-1)
    vis_rows = vis_index.reshape(MB, CAP)
    mask_rows = mask_index.reshape(MB, CAP)
    zero_rows = jnp.zeros((CAP, model_width), jnp.bfloat16)
    zero_matrix = jnp.zeros((model_width, hidden_width), jnp.float32)
    zero_down = jnp.zeros((hidden_width, model_width), jnp.float32)
    zero_enc = jnp.zeros(enc_vectors.shape, jnp.float32)
    zero_reg = jnp.zeros(reg_vectors.shape, jnp.float32)
    zero_mlp = jnp.zeros(mlp_vectors.shape, jnp.float32)
    zero_hidden = jnp.zeros(hidden_bias.shape, jnp.float32)

    def encoder_attention_step(incoming, feed_row, image_row, vis_row, mask_row):
        outcome, kept_values = encoder_attention(
            feed_row.astype(jnp.float32), matrix, enc_vectors, image_mask(image_row)
        )
        return (outcome.astype(jnp.bfloat16), zero_rows)

    def encoder_mlp_step(incoming, feed_row, image_row, vis_row, mask_row):
        outcome, kept_values = feed_forward(
            incoming.astype(jnp.float32), matrix, full_down, mlp_vectors[0], hidden_bias[0]
        )
        outgoing = outcome.astype(jnp.bfloat16)
        return (outgoing, outgoing)

    def regressor_attention_step(incoming, feed_row, image_row, vis_row, mask_row):
        outcome, kept_values = regressor_attention(
            incoming.astype(jnp.float32),
            feed_row.astype(jnp.float32),
            lookup(pos_table, vis_row),
            lookup(pos_table, mask_row),
            matrix,
            reg_vectors,
            image_keys(image_row),
        )
        return (outcome.astype(jnp.bfloat16), zero_rows)

    def regressor_mlp_step(incoming, feed_row, image_row, vis_row, mask_row):
        outcome, kept_values = feed_forward(
            incoming.astype(jnp.float32), matrix, full_down, mlp_vectors[1], hidden_bias[1]
        )
        outgoing = outcome.astype(jnp.bfloat16)
        return (outgoing, outgoing)

    def resting_step(incoming, feed_row, image_row, vis_row, mask_row):
        return (zero_rows, zero_rows)

    forward_branches = [
        encoder_attention_step,
        encoder_mlp_step,
        regressor_attention_step,
        regressor_mlp_step,
        resting_step,
    ]

    def encoder_attention_grads(stored_row, feed_row, incoming, image_row, vis_row, mask_row):
        d_residual, grad_matrix, grad_vectors = encoder_attention_back(
            incoming.astype(jnp.float32),
            feed_row.astype(jnp.float32),
            matrix,
            enc_vectors,
            image_mask(image_row),
        )
        return (
            zero_rows,
            d_residual.astype(jnp.bfloat16),
            grad_matrix,
            zero_down,
            grad_vectors,
            zero_reg,
            zero_mlp,
            zero_hidden,
        )

    def encoder_mlp_grads(stored_row, feed_row, incoming, image_row, vis_row, mask_row):
        gradient = feed_row.astype(jnp.float32) + incoming.astype(jnp.float32)
        d_residual, grad_up, grad_down, grad_vectors, grad_hidden = feed_forward_back(
            gradient,
            stored_row.astype(jnp.float32),
            matrix,
            full_down,
            mlp_vectors[0],
            hidden_bias[0],
        )
        return (
            d_residual.astype(jnp.bfloat16),
            zero_rows,
            grad_up,
            grad_down,
            zero_enc,
            zero_reg,
            zero_mlp.at[0].set(grad_vectors),
            zero_hidden.at[0].set(grad_hidden),
        )

    def regressor_attention_grads(stored_row, feed_row, incoming, image_row, vis_row, mask_row):
        d_latent, d_queries, grad_matrix, grad_vectors = regressor_attention_back(
            incoming.astype(jnp.float32),
            stored_row.astype(jnp.float32),
            feed_row.astype(jnp.float32),
            lookup(pos_table, vis_row),
            lookup(pos_table, mask_row),
            matrix,
            reg_vectors,
            image_keys(image_row),
        )
        return (
            d_latent.astype(jnp.bfloat16),
            d_queries.astype(jnp.bfloat16),
            grad_matrix,
            zero_down,
            zero_enc,
            grad_vectors,
            zero_mlp,
            zero_hidden,
        )

    def regressor_mlp_grads(stored_row, feed_row, incoming, image_row, vis_row, mask_row):
        d_residual, grad_up, grad_down, grad_vectors, grad_hidden = feed_forward_back(
            feed_row.astype(jnp.float32),
            stored_row.astype(jnp.float32),
            matrix,
            full_down,
            mlp_vectors[1],
            hidden_bias[1],
        )
        return (
            d_residual.astype(jnp.bfloat16),
            zero_rows,
            grad_up,
            grad_down,
            zero_enc,
            zero_reg,
            zero_mlp.at[1].set(grad_vectors),
            zero_hidden.at[1].set(grad_hidden),
        )

    def resting_grads(stored_row, feed_row, incoming, image_row, vis_row, mask_row):
        return (
            zero_rows,
            zero_rows,
            zero_matrix,
            zero_down,
            zero_enc,
            zero_reg,
            zero_mlp,
            zero_hidden,
        )

    backward_branches = [
        encoder_attention_grads,
        encoder_mlp_grads,
        regressor_attention_grads,
        regressor_mlp_grads,
        resting_grads,
    ]

    def forward_tick(moment, carried):
        incoming, back_incoming, saved_rows, results, grad_parts, totals = carried
        micro_index = moment - section_index
        is_active = (micro_index >= 0) & (micro_index < MB)
        row_slot = jnp.clip(micro_index, 0, MB - 1)
        outgoing, result_row = lax.switch(
            jnp.where(is_active, section_index, 4),
            forward_branches,
            incoming,
            pick_row(section_feed, row_slot),
            pick_row(images, row_slot),
            pick_row(vis_rows, row_slot),
            pick_row(mask_rows, row_slot),
        )
        saved_rows = put_row(
            saved_rows, jnp.where(is_active, incoming, pick_row(saved_rows, row_slot)), row_slot
        )
        keep_result = is_active & odd_section
        results = put_row(
            results, jnp.where(keep_result, result_row, pick_row(results, row_slot)), row_slot
        )
        incoming = jax.tree.map(
            lambda part, own: part.astype(own.dtype),
            shifted(shortened(outgoing), "section", 1),
            outgoing,
        )
        return (incoming, back_incoming, saved_rows, results, grad_parts, totals)

    def backward_tick(moment, carried):
        incoming, back_incoming, saved_rows, results, grad_parts, totals = carried
        micro_index = moment - (section_count - 1) + section_index
        is_active = (micro_index >= 0) & (micro_index < MB)
        row_slot = jnp.clip(micro_index, 0, MB - 1)
        produced = lax.switch(
            jnp.where(is_active, section_index, 4),
            backward_branches,
            pick_row(saved_rows, row_slot),
            pick_row(section_feed, row_slot),
            back_incoming,
            pick_row(images, row_slot),
            pick_row(vis_rows, row_slot),
            pick_row(mask_rows, row_slot),
        )
        outgoing, result_row, first_part, down_part = (
            produced[0],
            produced[1],
            produced[2],
            produced[3],
        )
        totals = tuple((earlier + later for earlier, later in zip(totals, produced[4:])))
        grad_parts = add_grads(grad_parts, first_part, down_part)
        keep_result = is_active & jnp.logical_not(odd_section)
        results = put_row(
            results, jnp.where(keep_result, result_row, pick_row(results, row_slot)), row_slot
        )
        back_incoming = jax.tree.map(
            lambda part, own: part.astype(own.dtype),
            shifted(shortened(outgoing), "section", -1),
            outgoing,
        )
        return (incoming, back_incoming, saved_rows, results, grad_parts, totals)

    grad_parts = (zero_matrix, zero_down)
    carried = (
        zero_rows,
        zero_rows,
        jnp.zeros((MB, CAP, model_width), jnp.bfloat16),
        jnp.zeros((MB, CAP, model_width), jnp.bfloat16),
        grad_parts,
        (zero_enc, zero_reg, zero_mlp, zero_hidden),
    )
    carried = lax.fori_loop(0, MB + section_count - 1, forward_tick, carried)
    carried = lax.fori_loop(0, MB + section_count - 1, backward_tick, carried)
    incoming, back_incoming, saved_rows, results, grad_parts, totals = carried
    own_first, own_down = settle(grad_parts[0], grad_parts[1], section_index)
    first_total, down_total = lax.psum((own_first, own_down), "dp")
    enc_total, reg_total, mlp_total, hidden_total = lax.psum(
        (totals[0], totals[1], totals[2], totals[3]), ("dp", "section")
    )
    spread_out = lax.all_to_all(
        results.reshape(1, MB * CAP, model_width),
        "section",
        split_axis=1,
        concat_axis=0,
        tiled=True,
    )
    return (
        spread_out[1],
        spread_out[3],
        spread_out[0],
        spread_out[2],
        first_total[None],
        down_total,
        enc_total,
        reg_total,
        mlp_total,
        hidden_total,
    )


def solution(mesh):
    in_specs = (
        P(("dp", "section"), None),
        P(("dp", "section"), None),
        P(("dp", "section"), None),
        P(("dp", "section"), None),
        P("section", None, None),
        P("section", None),
        P(),
        P(),
        P(),
        P(),
        P(),
        P("dp", None),
        P("dp"),
        P("dp"),
    )
    out_specs = (
        P(("dp", "section"), None),
        P(("dp", "section"), None),
        P(("dp", "section"), None),
        P(("dp", "section"), None),
        P("section", None, None),
        P("section", None),
        P(),
        P(),
        P(),
        P(),
    )
    return jax.shard_map(body, mesh=mesh, in_specs=in_specs, out_specs=out_specs, check_vma=False)
```

profile of v0, /device:TPU:0, one launch (start us, length us, event | category | flops | bytes accessed | tf_op | source)
XLA Modules:
  0.0 2054.8 jit_solution(13326742106057794266)
XLA Ops:
  51.2 394.9 %while.51 = (s32[]{:T(128)}, bf16[384,768]{1,0:T(8,128)(2,1)S(1)}, bf16[4,384,768]{2,1,0:T(8,128)(2,1)}, bf16[4,384,768]{2,1,0:T(8,128)(2,1)}, s32[]{:T(128)}, /...) while((s32[]{:T(128)}, bf16[384,768]{1,0:T(8,128)(2,1)S(1)}, ...), condition=%wide.region_24.25_spmd, body=%wide.region_2.24_spmd.sunk | while | flops 5944452096 | bytes 72285696 | solution.py:582
  52.7 39.3 %conditional.5 = (bf16[384,768]{1,0:T(8,128)(2,1)}, bf16[384,768]{1,0:T(8,128)(2,1)S(1)}) conditional(s32[]{:T(128)} %clamp.20, (bf16[384,768]{1,0:T(8,128)(2,1)S(1)}, f32[6,768]{1,0:T(8,128)}, bf16[768,3072]{1,0:T(8,128)(2,1)}, s32[384]{0:T(512)S(1)}) %tuple.260, (bf16[384,768]{1,0:T(8,128)(2,1)S(1)}, ...), branch_computations={%region_3.7_spmd, %region_8.10_spmd, %region_11.19_spmd, %region_2... | conditional | flops 5943862272 | bytes 61664816 | solution.py:516
  109.8 39.2 %conditional.5 = (bf16[384,768]{1,0:T(8,128)(2,1)}, bf16[384,768]{1,0:T(8,128)(2,1)S(1)}) conditional(s32[]{:T(128)} %clamp.20, (bf16[384,768]{1,0:T(8,128)(2,1)S(1)}, f32[6,768]{1,0:T(8,128)}, bf16[768,3072]{1,0:T(8,128)(2,1)}, s32[384]{0:T(512)S(1)}) %tuple.260, (bf16[384,768]{1,0:T(8,128)(2,1)S(1)}, ...), branch_computations={%region_3.7_spmd, %region_8.10_spmd, %region_11.19_spmd, %region_2... | conditional | flops 5943862272 | bytes 61664816 | solution.py:516
  155.4 39.1 %conditional.5 = (bf16[384,768]{1,0:T(8,128)(2,1)}, bf16[384,768]{1,0:T(8,128)(2,1)S(1)}) conditional(s32[]{:T(128)} %clamp.20, (bf16[384,768]{1,0:T(8,128)(2,1)S(1)}, f32[6,768]{1,0:T(8,128)}, bf16[768,3072]{1,0:T(8,128)(2,1)}, s32[384]{0:T(512)S(1)}) %tuple.260, (bf16[384,768]{1,0:T(8,128)(2,1)S(1)}, ...), branch_computations={%region_3.7_spmd, %region_8.10_spmd, %region_11.19_spmd, %region_2... | conditional | flops 5943862272 | bytes 61664816 | solution.py:516
  200.9 34.3 %conditional.5 = (bf16[384,768]{1,0:T(8,128)(2,1)}, bf16[384,768]{1,0:T(8,128)(2,1)S(1)}) conditional(s32[]{:T(128)} %clamp.20, (bf16[384,768]{1,0:T(8,128)(2,1)S(1)}, f32[6,768]{1,0:T(8,128)}, bf16[768,3072]{1,0:T(8,128)(2,1)}, s32[384]{0:T(512)S(1)}) %tuple.260, (bf16[384,768]{1,0:T(8,128)(2,1)S(1)}, ...), branch_computations={%region_3.7_spmd, %region_8.10_spmd, %region_11.19_spmd, %region_2... | conditional | flops 5943862272 | bytes 61664816 | solution.py:516
  262.1 32.5 %conditional.5 = (bf16[384,768]{1,0:T(8,128)(2,1)}, bf16[384,768]{1,0:T(8,128)(2,1)S(1)}) conditional(s32[]{:T(128)} %clamp.20, (bf16[384,768]{1,0:T(8,128)(2,1)S(1)}, f32[6,768]{1,0:T(8,128)}, bf16[768,3072]{1,0:T(8,128)(2,1)}, s32[384]{0:T(512)S(1)}) %tuple.260, (bf16[384,768]{1,0:T(8,128)(2,1)S(1)}, ...), branch_computations={%region_3.7_spmd, %region_8.10_spmd, %region_11.19_spmd, %region_2... | conditional | flops 5943862272 | bytes 61664816 | solution.py:516
  323.8 32.9 %conditional.5 = (bf16[384,768]{1,0:T(8,128)(2,1)}, bf16[384,768]{1,0:T(8,128)(2,1)S(1)}) conditional(s32[]{:T(128)} %clamp.20, (bf16[384,768]{1,0:T(8,128)(2,1)S(1)}, f32[6,768]{1,0:T(8,128)}, bf16[768,3072]{1,0:T(8,128)(2,1)}, s32[384]{0:T(512)S(1)}) %tuple.260, (bf16[384,768]{1,0:T(8,128)(2,1)S(1)}, ...), branch_computations={%region_3.7_spmd, %region_8.10_spmd, %region_11.19_spmd, %region_2... | conditional | flops 5943862272 | bytes 61664816 | solution.py:516
  379.6 32.6 %conditional.5 = (bf16[384,768]{1,0:T(8,128)(2,1)}, bf16[384,768]{1,0:T(8,128)(2,1)S(1)}) conditional(s32[]{:T(128)} %clamp.20, (bf16[384,768]{1,0:T(8,128)(2,1)S(1)}, f32[6,768]{1,0:T(8,128)}, bf16[768,3072]{1,0:T(8,128)(2,1)}, s32[384]{0:T(512)S(1)}) %tuple.260, (bf16[384,768]{1,0:T(8,128)(2,1)S(1)}, ...), branch_computations={%region_3.7_spmd, %region_8.10_spmd, %region_11.19_spmd, %region_2... | conditional | flops 5943862272 | bytes 61664816 | solution.py:516
  412.2 29.0 %collective-permute-start = (bf16[384,768]{1,0:T(8,128)(2,1)}, bf16[384,768]{1,0:T(8,128)(2,1)S(1)}, u32[]{:S(2)}, u32[]{:S(2)}) collective-permute-start(bf16[384,768]{1,0:T(8,128)(2,1)} %get-tuple-element.1797), channel_id=1, source_target_pairs={{0,1},{1,2},{2,3},{4,5},{5,6},{6,7},{8,9},{9,10},{10,11},{12,13},{... | collective-permute-start | bytes 1769480 | tf_op jit(solution)/shard_map/while/body/eval_jaxpr/ppermute | solution.py:22
  446.1 1005.2 %while.52 = (s32[]{:T(128)}, bf16[384,768]{1,0:T(8,128)(2,1)S(1)}, bf16[4,384,768]{2,1,0:T(8,128)(2,1)}, f32[768,3072]{0,1:T(8,128)}, f32[3072,768]{1,0:T(8,128)...) while((s32[]{:T(128)}, bf16[384,768]{1,0:T(8,128)(2,1)S(1)}, ...), condition=%wide.region_87.88_spmd.clone, body=%wide.region_25.87_spmd.clone.sunk | while | flops 13744031744 | bytes 451778752 | solution.py:583
  452.1 47.1 %conditional.6 = (bf16[384,768]{1,0:T(8,128)(2,1)}, bf16[384,768]{1,0:T(8,128)(2,1)}, f32[768,3072]{0,1:T(8,128)}, f32[3072,768]{1,0:T(8,128)}, f32[6,768]{1,0:T...) conditional(s32[]{:T(128)} %clamp.21, ...), branch_computations={%region_26.39_spmd, %region_40.49_spmd, %region_50.75_spmd, %regio... | conditional | flops 13734250496 | bytes 379839808 | solution.py:544
  523.4 47.1 %conditional.6 = (bf16[384,768]{1,0:T(8,128)(2,1)}, bf16[384,768]{1,0:T(8,128)(2,1)}, f32[768,3072]{0,1:T(8,128)}, f32[3072,768]{1,0:T(8,128)}, f32[6,768]{1,0:T...) conditional(s32[]{:T(128)} %clamp.21, ...), branch_computations={%region_26.39_spmd, %region_40.49_spmd, %region_50.75_spmd, %regio... | conditional | flops 13734250496 | bytes 379839808 | solution.py:544
  600.1 47.1 %conditional.6 = (bf16[384,768]{1,0:T(8,128)(2,1)}, bf16[384,768]{1,0:T(8,128)(2,1)}, f32[768,3072]{0,1:T(8,128)}, f32[3072,768]{1,0:T(8,128)}, f32[6,768]{1,0:T...) conditional(s32[]{:T(128)} %clamp.21, ...), branch_computations={%region_26.39_spmd, %region_40.49_spmd, %region_50.75_spmd, %regio... | conditional | flops 13734250496 | bytes 379839808 | solution.py:544
  673.5 101.6 %collective-permute-done.1 = bf16[384,768]{1,0:T(8,128)(2,1)S(1)} collective-permute-done((bf16[384,768]{1,0:T(8,128)(2,1)}, bf16[384,768]{1,0:T(8,128)(2,1)S(1)}, u32[]{:S(2)}, u32[]{:S(2)}) %collective-permute-start.1) | collective-permute-done | bytes 589856 | tf_op jit(solution)/shard_map/while/body/eval_jaxpr/ppermute | solution.py:22
  777.8 102.9 %conditional.6 = (bf16[384,768]{1,0:T(8,128)(2,1)}, bf16[384,768]{1,0:T(8,128)(2,1)}, f32[768,3072]{0,1:T(8,128)}, f32[3072,768]{1,0:T(8,128)}, f32[6,768]{1,0:T...) conditional(s32[]{:T(128)} %clamp.21, ...), branch_computations={%region_26.39_spmd, %region_40.49_spmd, %region_50.75_spmd, %regio... | conditional | flops 13734250496 | bytes 379839808 | solution.py:544
  907.0 47.2 %collective-permute-done.1 = bf16[384,768]{1,0:T(8,128)(2,1)S(1)} collective-permute-done((bf16[384,768]{1,0:T(8,128)(2,1)}, bf16[384,768]{1,0:T(8,128)(2,1)S(1)}, u32[]{:S(2)}, u32[]{:S(2)}) %collective-permute-start.1) | collective-permute-done | bytes 589856 | tf_op jit(solution)/shard_map/while/body/eval_jaxpr/ppermute | solution.py:22
  956.8 102.9 %conditional.6 = (bf16[384,768]{1,0:T(8,128)(2,1)}, bf16[384,768]{1,0:T(8,128)(2,1)}, f32[768,3072]{0,1:T(8,128)}, f32[3072,768]{1,0:T(8,128)}, f32[6,768]{1,0:T...) conditional(s32[]{:T(128)} %clamp.21, ...), branch_computations={%region_26.39_spmd, %region_40.49_spmd, %region_50.75_spmd, %regio... | conditional | flops 13734250496 | bytes 379839808 | solution.py:544
  1086.1 46.9 %collective-permute-done.1 = bf16[384,768]{1,0:T(8,128)(2,1)S(1)} collective-permute-done((bf16[384,768]{1,0:T(8,128)(2,1)}, bf16[384,768]{1,0:T(8,128)(2,1)S(1)}, u32[]{:S(2)}, u32[]{:S(2)}) %collective-permute-start.1) | collective-permute-done | bytes 589856 | tf_op jit(solution)/shard_map/while/body/eval_jaxpr/ppermute | solution.py:22
  1135.6 102.9 %conditional.6 = (bf16[384,768]{1,0:T(8,128)(2,1)}, bf16[384,768]{1,0:T(8,128)(2,1)}, f32[768,3072]{0,1:T(8,128)}, f32[3072,768]{1,0:T(8,128)}, f32[6,768]{1,0:T...) conditional(s32[]{:T(128)} %clamp.21, ...), branch_computations={%region_26.39_spmd, %region_40.49_spmd, %region_50.75_spmd, %regio... | conditional | flops 13734250496 | bytes 379839808 | solution.py:544
  1264.9 47.4 %collective-permute-done.1 = bf16[384,768]{1,0:T(8,128)(2,1)S(1)} collective-permute-done((bf16[384,768]{1,0:T(8,128)(2,1)}, bf16[384,768]{1,0:T(8,128)(2,1)S(1)}, u32[]{:S(2)}, u32[]{:S(2)}) %collective-permute-start.1) | collective-permute-done | bytes 589856 | tf_op jit(solution)/shard_map/while/body/eval_jaxpr/ppermute | solution.py:22
  1314.8 102.9 %conditional.6 = (bf16[384,768]{1,0:T(8,128)(2,1)}, bf16[384,768]{1,0:T(8,128)(2,1)}, f32[768,3072]{0,1:T(8,128)}, f32[3072,768]{1,0:T(8,128)}, f32[6,768]{1,0:T...) conditional(s32[]{:T(128)} %clamp.21, ...), branch_computations={%region_26.39_spmd, %region_40.49_spmd, %region_50.75_spmd, %regio... | conditional | flops 13734250496 | bytes 379839808 | solution.py:544
  1472.3 33.6 %copy.155 = bf16[1,1536,768]{2,0,1:T(2,128)(2,1)} copy(bf16[1,1536,768]{2,1,0:T(8,128)(2,1)S(1)} %bitcast.205) | data formatting | bytes 4718592 | tf_op jit(solution)/shard_map/reshape | solution.py:591
  1532.7 51.5 %all_to_all.21 = bf16[4,2,147456]{2,1,0:T(2,128)(2,1)S(1)} all-to-all(bf16[4,2,147456]{2,1,0:T(2,128)(2,1)} %reshape.688), channel_id=1, replica_groups=mesh['dp'=8,'section'=4] {'section'}, dimensions={0} | all-to-all | bytes 4718592 | tf_op jit(solution)/shard_map/all_to_all | solution.py:590
  1598.1 436.2 %all-reduce.11.cloned.1.call-done = (f32[1,768,3072]{2,1,0:T(8,128)}, f32[1536,768]{1,0:T(8,128)}) async-done(((f32[1,768,3072]{2,1,0:T(8,128)}, f32[1536,768]{1,0:T(8,128)}), (f32[1,768,3072]{2,1,0:T(8,128)}, f32[1536,768]{1,0:T(8,128)})) %all-reduce.11.cloned.1.call-update) | async-done | bytes 14155792 | tf_op jit(solution)/shard_map/psum | solution.py:586
  (943 shorter events, 882.0 us)
Async XLA Ops:
  7.2 11.3 collective-permute-start.2
  14.2 32.2 %all-to-all-start = ((bf16[4,384,768]{2,1,0:T(8,128)(2,1)}), bf16[4,384,768]{2,1,0:T(8,128)(2,1)S(1)}, u32[]{:S(2)}, u32[]{:S(2)}) async-start(bf16[4,384,768]{2,1,0:T(8,128)(2,1)} %pad_maximum_fusion.9), calls=%async_computation | async-start | bytes 4718592 | tf_op jit(solution)/shard_map/all_to_all | solution.py:349
  18.0 1580.1 %all-reduce.9.cloned.1.call-start = ((), (), s32[]{:S(2)}) async-start(), calls=%async_computation.2 | async-start | bytes 245760 | tf_op jit(solution)/shard_map/psum | solution.py:587
  92.0 16.2 collective-permute-start
  149.0 4.9 collective-permute-start
  194.5 4.9 collective-permute-start
  235.2 25.2 %collective-permute-start = (bf16[384,768]{1,0:T(8,128)(2,1)}, bf16[384,768]{1,0:T(8,128)(2,1)S(1)}, u32[]{:S(2)}, u32[]{:S(2)}) collective-permute-start(bf16[384,768]{1,0:T(8,128)(2,1)} %get-tuple-element.1797), channel_id=1, source_target_pairs={{0,1},{1,2},{2,3},{4,5},{5,6},{6,7},{8,9},{9,10},{10,11},{12,13},{... | collective-permute-start | bytes 1769480 | tf_op jit(solution)/shard_map/while/body/eval_jaxpr/ppermute | solution.py:22
  294.7 27.7 %collective-permute-start = (bf16[384,768]{1,0:T(8,128)(2,1)}, bf16[384,768]{1,0:T(8,128)(2,1)S(1)}, u32[]{:S(2)}, u32[]{:S(2)}) collective-permute-start(bf16[384,768]{1,0:T(8,128)(2,1)} %get-tuple-element.1797), channel_id=1, source_target_pairs={{0,1},{1,2},{2,3},{4,5},{5,6},{6,7},{8,9},{9,10},{10,11},{12,13},{... | collective-permute-start | bytes 1769480 | tf_op jit(solution)/shard_map/while/body/eval_jaxpr/ppermute | solution.py:22
  356.7 21.5 %collective-permute-start = (bf16[384,768]{1,0:T(8,128)(2,1)}, bf16[384,768]{1,0:T(8,128)(2,1)S(1)}, u32[]{:S(2)}, u32[]{:S(2)}) collective-permute-start(bf16[384,768]{1,0:T(8,128)(2,1)} %get-tuple-element.1797), channel_id=1, source_target_pairs={{0,1},{1,2},{2,3},{4,5},{5,6},{6,7},{8,9},{9,10},{10,11},{12,13},{... | collective-permute-start | bytes 1769480 | tf_op jit(solution)/shard_map/while/body/eval_jaxpr/ppermute | solution.py:22
  412.2 32.7 %collective-permute-start = (bf16[384,768]{1,0:T(8,128)(2,1)}, bf16[384,768]{1,0:T(8,128)(2,1)S(1)}, u32[]{:S(2)}, u32[]{:S(2)}) collective-permute-start(bf16[384,768]{1,0:T(8,128)(2,1)} %get-tuple-element.1797), channel_id=1, source_target_pairs={{0,1},{1,2},{2,3},{4,5},{5,6},{6,7},{8,9},{9,10},{10,11},{12,13},{... | collective-permute-start | bytes 1769480 | tf_op jit(solution)/shard_map/while/body/eval_jaxpr/ppermute | solution.py:22
  499.3 20.9 %collective-permute-start.1 = (bf16[384,768]{1,0:T(8,128)(2,1)}, bf16[384,768]{1,0:T(8,128)(2,1)S(1)}, u32[]{:S(2)}, u32[]{:S(2)}) collective-permute-start(bf16[384,768]{1,0:T(8,128)(2,1)} %get-tuple-element.1826), channel_id=1, source_target_pairs={{1,0},{2,1},{3,2},{5,4},{6,5},{7,6},{9,8},{10,9},{11,10},{13,12},{... | collective-permute-start | bytes 1769480 | tf_op jit(solution)/shard_map/while/body/eval_jaxpr/ppermute | solution.py:22
  570.6 26.3 %collective-permute-start.1 = (bf16[384,768]{1,0:T(8,128)(2,1)}, bf16[384,768]{1,0:T(8,128)(2,1)S(1)}, u32[]{:S(2)}, u32[]{:S(2)}) collective-permute-start(bf16[384,768]{1,0:T(8,128)(2,1)} %get-tuple-element.1826), channel_id=1, source_target_pairs={{1,0},{2,1},{3,2},{5,4},{6,5},{7,6},{9,8},{10,9},{11,10},{13,12},{... | collective-permute-start | bytes 1769480 | tf_op jit(solution)/shard_map/while/body/eval_jaxpr/ppermute | solution.py:22
  647.2 127.9 %collective-permute-start.1 = (bf16[384,768]{1,0:T(8,128)(2,1)}, bf16[384,768]{1,0:T(8,128)(2,1)S(1)}, u32[]{:S(2)}, u32[]{:S(2)}) collective-permute-start(bf16[384,768]{1,0:T(8,128)(2,1)} %get-tuple-element.1826), channel_id=1, source_target_pairs={{1,0},{2,1},{3,2},{5,4},{6,5},{7,6},{9,8},{10,9},{11,10},{13,12},{... | collective-permute-start | bytes 1769480 | tf_op jit(solution)/shard_map/while/body/eval_jaxpr/ppermute | solution.py:22
  661.0 114.1 %copy-start.36 = (f32[2,4,768]{2,1,0:T(4,128)S(1)}, f32[2,4,768]{2,1,0:T(4,128)}, u32[]{:S(2)}) copy-start(f32[2,4,768]{2,1,0:T(4,128)} %copy-done.35) | copy-start | bytes 73732 | tf_op jit(solution)/shard_map/while
  661.0 114.1 %copy-start.39 = (f32[2,3072]{1,0:T(2,128)S(1)}, f32[2,3072]{1,0:T(2,128)}, u32[]{:S(2)}) copy-start(f32[2,3072]{1,0:T(2,128)} %copy-done.38) | copy-start | bytes 73732 | tf_op jit(solution)/shard_map/while
  661.1 114.1 %copy-start.92 = (s32[4,384]{1,0:T(4,128)S(1)}, s32[4,384]{1,0:T(4,128)}, u32[]{:S(2)}) copy-start(s32[4,384]{1,0:T(4,128)} %copy-done.91) | copy-start | bytes 18436 | tf_op jit(solution)/shard_map/while
  661.1 114.1 %copy-start.94 = (s32[4,384]{1,0:T(4,128)S(1)}, s32[4,384]{1,0:T(4,128)}, u32[]{:S(2)}) copy-start(s32[4,384]{1,0:T(4,128)} %copy-done.93) | copy-start | bytes 18436 | tf_op jit(solution)/shard_map/while
  661.1 114.1 %copy-start.96 = (s32[4,384]{1,0:T(4,128)S(1)}, s32[4,384]{1,0:T(4,128)}, u32[]{:S(2)}) copy-start(s32[4,384]{1,0:T(4,128)} %copy-done.95) | copy-start | bytes 18436 | tf_op jit(solution)/shard_map/while
  880.7 73.5 %collective-permute-start.1 = (bf16[384,768]{1,0:T(8,128)(2,1)}, bf16[384,768]{1,0:T(8,128)(2,1)S(1)}, u32[]{:S(2)}, u32[]{:S(2)}) collective-permute-start(bf16[384,768]{1,0:T(8,128)(2,1)} %get-tuple-element.1826), channel_id=1, source_target_pairs={{1,0},{2,1},{3,2},{5,4},{6,5},{7,6},{9,8},{10,9},{11,10},{13,12},{... | collective-permute-start | bytes 1769480 | tf_op jit(solution)/shard_map/while/body/eval_jaxpr/ppermute | solution.py:22
  1059.8 73.2 %collective-permute-start.1 = (bf16[384,768]{1,0:T(8,128)(2,1)}, bf16[384,768]{1,0:T(8,128)(2,1)S(1)}, u32[]{:S(2)}, u32[]{:S(2)}) collective-permute-start(bf16[384,768]{1,0:T(8,128)(2,1)} %get-tuple-element.1826), channel_id=1, source_target_pairs={{1,0},{2,1},{3,2},{5,4},{6,5},{7,6},{9,8},{10,9},{11,10},{13,12},{... | collective-permute-start | bytes 1769480 | tf_op jit(solution)/shard_map/while/body/eval_jaxpr/ppermute | solution.py:22
  1238.5 73.7 %collective-permute-start.1 = (bf16[384,768]{1,0:T(8,128)(2,1)}, bf16[384,768]{1,0:T(8,128)(2,1)S(1)}, u32[]{:S(2)}, u32[]{:S(2)}) collective-permute-start(bf16[384,768]{1,0:T(8,128)(2,1)} %get-tuple-element.1826), channel_id=1, source_target_pairs={{1,0},{2,1},{3,2},{5,4},{6,5},{7,6},{9,8},{10,9},{11,10},{13,12},{... | collective-permute-start | bytes 1769480 | tf_op jit(solution)/shard_map/while/body/eval_jaxpr/ppermute | solution.py:22
  1417.8 26.3 %collective-permute-start.1 = (bf16[384,768]{1,0:T(8,128)(2,1)}, bf16[384,768]{1,0:T(8,128)(2,1)S(1)}, u32[]{:S(2)}, u32[]{:S(2)}) collective-permute-start(bf16[384,768]{1,0:T(8,128)(2,1)} %get-tuple-element.1826), channel_id=1, source_target_pairs={{1,0},{2,1},{3,2},{5,4},{6,5},{7,6},{9,8},{10,9},{11,10},{13,12},{... | collective-permute-start | bytes 1769480 | tf_op jit(solution)/shard_map/while/body/eval_jaxpr/ppermute | solution.py:22
  1453.9 11.0 collective-permute-start.3
  1464.9 569.4 %all-reduce.11.cloned.1.call-start = ((), (), s32[]{:S(2)}) async-start(), calls=%async_computation.3 | async-start | bytes 28311552 | tf_op jit(solution)/shard_map/psum | solution.py:586
  (245 other events, 3240.7 us)
Sparse Core Ops, SparseCore 0:
  1465.0 126.2 all-reduce.8
  1596.1 438.1 all-reduce.10
where the time goes:
time: 2060 us; the launch traced here: 2050 us
  waiting for transfers between devices  702 us (34%)
  loops' own time  365 us (18%)
  local copies, waits for them, and re-layouts  292 us (14%)
  other arithmetic  275 us (13%)
  matrix products  229 us (11%)
  starting transfers between devices  126 us (6%)
  blocking collectives  51.5 us (2%)
    psum x1, waiting for transfers between devices, body(): first_total, down_total = lax.psum((own_first, own_down), 'dp')  436 us
    ppermute x16, waiting for transfers between devices, shifted(): return lax.ppermute(block, axis, route)  243 us
    another operation x7, loops' own time, backward_tick(): lax.switch(jnp.where(is_active, section_index, 4), backward_branches, pic...  194 us
    add x14, other arithmetic, add_grads(): return (grad_parts[0] + first_part, grad_parts[1] + down_part)  153 us
    another operation x7, loops' own time, forward_tick(): lax.switch(jnp.where(is_active, section_index, 4), forward_branches, inco...  151 us
    ppermute x16, starting transfers between devices, shifted(): return lax.ppermute(block, axis, route)  122 us
    all_to_all x1, blocking collectives, body(): lax.all_to_all(results.reshape(1, MB * CAP, model_width), 'section', spli...  51.5 us
    sub x8, matrix products, attention_core(): raised = jnp.exp(scores - highest)  47 us
  transfers between devices with their start and end apart: 19, of which 6 were waited for; matrix products, arithmetic and copies ran while one was open for 14% of the time, Pallas kernels for 0%

commit v1 on v0

v1 whole, which is shorter than its diff:
```python
import functools

import jax
import jax.numpy as jnp
from jax import lax
from jax.experimental import pallas as pl
from jax.experimental.pallas import tpu as pltpu
from jax.sharding import PartitionSpec as P

F32 = jnp.float32
BF16 = jnp.bfloat16
CAP = 384
IMGS = 4
SLOT = 128
PAD = IMGS * SLOT
D = 768
FF = 3072
LANES = 128
PAIRS = D // LANES
HB = 512
EPS = 1e-06
MIB = 1 << 20
ANY = pl.BlockSpec(memory_space=pl.ANY)
SMEM = pl.BlockSpec(memory_space=pltpu.SMEM)


def params(limit=48, **more):
    return pltpu.CompilerParams(vmem_limit_bytes=limit * MIB, **more)


def sds(shape, dtype):
    return jax.ShapeDtypeStruct(shape, dtype)


def dot(a, b):
    return jnp.dot(a, b, preferred_element_type=F32)


def dot_nt(a, b):
    return lax.dot_general(a, b, (((1,), (1,)), ((), ())), preferred_element_type=F32)


def dot_tn(a, b):
    return lax.dot_general(a, b, (((0,), (0,)), ((), ())), preferred_element_type=F32)


def row(ref, i):
    return ref[i : i + 1, :]


def colsum(values):
    return jnp.sum(values, axis=0, keepdims=True)


def normalize(values):
    centred = values - jnp.mean(values, axis=-1, keepdims=True)
    spread = jnp.mean(centred * centred, axis=-1, keepdims=True)
    inverse = lax.rsqrt(spread + EPS)
    return centred * inverse, inverse


def norm_back(gradient, gain, normed, inverse):
    scaled = gradient * gain
    level = jnp.mean(scaled, axis=-1, keepdims=True)
    slope = jnp.mean(scaled * normed, axis=-1, keepdims=True)
    return inverse * (scaled - level - normed * slope)


def gelu_parts(t):
    e = jnp.exp(-0.5 * t * t)
    k = 1.0 / (1.0 + (0.3275911 * 0.7071067811865476) * jnp.abs(t))
    poly = k * (
        0.127414796
        + k * (-0.142248368 + k * (0.7107068705 + k * (-0.7265760135 + k * 0.5307027145)))
    )
    tail = poly * e
    phi = jnp.where(t >= 0.0, 1.0 - tail, tail)
    return t * phi, phi + t * (e * 0.3989422804014327)


def image_bounds(lens, pack):
    sizes = [lens[pack, j] for j in range(IMGS)]
    starts = [jnp.int32(0)]
    for j in range(IMGS - 1):
        starts.append(starts[-1] + sizes[j])
    return starts, sizes


def pick_image(slots, values):
    image = lax.shift_right_logical(slots, 7)
    out = jnp.where(image == 1, values[1], values[0])
    out = jnp.where(image == 2, values[2], out)
    return jnp.where(image == 3, values[3], out)


def regroup_matrix(lens, pack):
    starts, sizes = image_bounds(lens, pack)
    slots = lax.broadcasted_iota(jnp.int32, (PAD, CAP), 0)
    rows = lax.broadcasted_iota(jnp.int32, (PAD, CAP), 1)
    place = lax.bitwise_and(slots, SLOT - 1)
    wanted = pick_image(slots, starts) + place
    hit = (wanted == rows) & (place < pick_image(slots, sizes))
    return jnp.where(hit, 1.0, 0.0).astype(BF16)


def ungroup_matrix(lens, pack):
    starts, sizes = image_bounds(lens, pack)
    rows = lax.broadcasted_iota(jnp.int32, (CAP, PAD), 0)
    slots = lax.broadcasted_iota(jnp.int32, (CAP, PAD), 1)
    place = lax.bitwise_and(slots, SLOT - 1)
    wanted = pick_image(slots, starts) + place
    hit = (wanted == rows) & (place < pick_image(slots, sizes))
    return jnp.where(hit, 1.0, 0.0).astype(BF16)


def lane_halves():
    lane = lax.broadcasted_iota(jnp.int32, (1, LANES), 1)
    first = jnp.where(lane < LANES // 2, 1.0, 0.0)
    return first.astype(BF16), (1.0 - first).astype(BF16)


def both_heads(block, halves):
    return jnp.concatenate([block * halves[0], block * halves[1]], axis=0)


def merge_heads(stacked):
    keys = stacked.shape[0] // 2
    lane = lax.broadcasted_iota(jnp.int32, (keys, LANES), 1)
    return jnp.where(lane < LANES // 2, stacked[:keys], stacked[keys:])


def softmax(scores):
    raised = jnp.exp(scores - jnp.max(scores, axis=-1, keepdims=True))
    return raised * (1.0 / jnp.sum(raised, axis=-1, keepdims=True))


def attend(lens, pack, packed, probs, mixed_slots, parts):
    halves = lane_halves()
    keys = SLOT * parts

    def image(j, carry):
        rows = pl.ds(pl.multiple_of(j * SLOT, SLOT), SLOT)
        size = lens[pack, j]
        place = lax.bitwise_and(
            lax.broadcasted_iota(jnp.int32, (SLOT, 2 * keys), 1), SLOT - 1
        )
        valid = place < size
        for g in range(PAIRS):
            cols = slice(g * LANES, (g + 1) * LANES)
            kk = jnp.concatenate([packed[1 + 2 * m, rows, cols] for m in range(parts)], axis=0)
            vv = jnp.concatenate([packed[2 + 2 * m, rows, cols] for m in range(parts)], axis=0)
            scores = dot_nt(packed[0, rows, cols], both_heads(kk, halves))
            scores = jnp.where(valid, scores, -1e30)
            prob = jnp.concatenate(
                [softmax(scores[:, :keys]), softmax(scores[:, keys:])], axis=1
            ).astype(BF16)
            probs[j, g] = prob
            mixed_slots[rows, cols] = dot(prob, both_heads(vv, halves)).astype(BF16)
        return carry

    lax.fori_loop(0, IMGS, image, 0)


def attend_back(packed, probs, d_mixed_slots, d_packed, parts):
    halves = lane_halves()
    keys = SLOT * parts

    def image(j, carry):
        rows = pl.ds(pl.multiple_of(j * SLOT, SLOT), SLOT)
        for g in range(PAIRS):
            cols = slice(g * LANES, (g + 1) * LANES)
            q = packed[0, rows, cols]
            kk = jnp.concatenate([packed[1 + 2 * m, rows, cols] for m in range(parts)], axis=0)
            vv = jnp.concatenate([packed[2 + 2 * m, rows, cols] for m in range(parts)], axis=0)
            d_out = d_mixed_slots[rows, cols]
            low = probs[j, g]
            prob = low.astype(F32)
            d_prob = dot_nt(d_out, both_heads(vv, halves))
            weighted = prob * d_prob
            d_scores = []
            for half in (slice(0, keys), slice(keys, 2 * keys)):
                centre = jnp.sum(weighted[:, half], axis=-1, keepdims=True)
                d_scores.append(weighted[:, half] - prob[:, half] * centre)
            d_scores = jnp.concatenate(d_scores, axis=1).astype(BF16)
            d_q = dot(d_scores, both_heads(kk, halves)) * 0.125
            d_packed[0, rows, cols] = d_q.astype(BF16)
            d_k = merge_heads(dot_tn(d_scores, q)).astype(BF16)
            d_v = merge_heads(dot_tn(low, d_out)).astype(BF16)
            for m in range(parts):
                part = slice(m * SLOT, (m + 1) * SLOT)
                d_packed[1 + 2 * m, rows, cols] = d_k[part]
                d_packed[2 + 2 * m, rows, cols] = d_v[part]
        return carry

    lax.fori_loop(0, IMGS, image, 0)


def blocks_of(i):
    return slice(i * D, (i + 1) * D)


ATT_STATE = (
    sds((5, CAP, D), BF16),
    sds((5, PAD, D), BF16),
    sds((IMGS, PAIRS, SLOT, 4 * SLOT), BF16),
    sds((CAP, D), BF16),
    sds((CAP, D), BF16),
    sds((CAP, D), F32),
    sds((CAP, D), F32),
)
FFN_STATE = (
    sds((CAP, D), BF16),
    sds((CAP, FF), BF16),
    sds((CAP, FF), BF16),
    sds((CAP, D), BF16),
)
ATT_GRADS = (
    sds((5, CAP, D), BF16),
    sds((CAP, D), BF16),
    sds((10, D), F32),
)
FFN_GRADS = (
    sds((CAP, FF), BF16),
    sds((CAP, D), BF16),
    sds((4, D), F32),
    sds((1, FF), F32),
)
ROWS = sds((CAP, D), BF16)


def full(shape):
    return pl.BlockSpec(shape, lambda i: (0,) * len(shape))


def lead(count, shape):
    return pl.BlockSpec((count, *shape), lambda i: (0,) * (1 + len(shape)))


def slot_of(index, shape):
    return pl.BlockSpec((None, *shape), lambda i: (index,) + (0,) * len(shape))


def unset(shapes):
    def kernel(*refs):
        del refs

    return pl.pallas_call(
        kernel, out_shape=shapes, out_specs=tuple(ANY for _ in shapes), name="unset"
    )()


def encoder_attention_kernel(
    lens, which, x, matrix, e, out, normed, packed, probs, mixed, branch, q_source, k_source, flat, mixed_slots
):
    del q_source, k_source
    pack = which[0]
    values = x[...].astype(F32)
    centred, _ = normalize(values)
    normed[0] = (centred * row(e, 0) + row(e, 1)).astype(BF16)
    flat[0] = ((dot(normed[0], matrix[:, blocks_of(0)]) + row(e, 2)).astype(BF16) * 0.125).astype(BF16)
    flat[1] = dot(normed[0], matrix[:, blocks_of(1)]).astype(BF16)
    flat[2] = (dot(normed[0], matrix[:, blocks_of(2)]) + row(e, 3)).astype(BF16)
    regroup = regroup_matrix(lens, pack)
    for m in range(3):
        packed[m] = dot(regroup, flat[m]).astype(BF16)
    attend(lens, pack, packed, probs, mixed_slots, 1)
    mixed[...] = dot(ungroup_matrix(lens, pack), mixed_slots[...]).astype(BF16)
    total = dot_nt(mixed[...], matrix[:, blocks_of(3)]) + row(e, 4)
    branch[...] = total.astype(BF16)
    out[...] = (values + row(e, 5) * total).astype(BF16)


def encoder_attention(lens, which, x, matrices, e):
    return pl.pallas_call(
        encoder_attention_kernel,
        grid=(1,),
        in_specs=[SMEM, SMEM, full((CAP, D)), slot_of(0, (D, FF)), full((6, D))],
        out_specs=(
            full((CAP, D)),
            lead(1, (CAP, D)),
            lead(3, (PAD, D)),
            full((IMGS, PAIRS, SLOT, 2 * SLOT)),
            full((CAP, D)),
            full((CAP, D)),
            ANY,
            ANY,
        ),
        out_shape=(ROWS, *ATT_STATE),
        scratch_shapes=[pltpu.VMEM((3, CAP, D), BF16), pltpu.VMEM((PAD, D), BF16)],
        compiler_params=params(),
        name="encoder_attention",
    )(lens, which, x, matrices, e)


def encoder_attention_back_kernel(
    lens, which, g_in, x, matrix, e, packed, probs, branch, d_x, d_flat, d_branch, vectors, d_slots, d_packed
):
    pack = which[0]
    g = g_in[...].astype(F32)
    vectors[5:6] = colsum(g * branch[...].astype(F32))
    d_branch[...] = (g * row(e, 5)).astype(BF16)
    vectors[4:5] = colsum(d_branch[...].astype(F32))
    d_mixed = dot(d_branch[...], matrix[:, blocks_of(3)]).astype(BF16)
    d_slots[...] = dot(regroup_matrix(lens, pack), d_mixed).astype(BF16)
    attend_back(packed, probs, d_slots, d_packed, 1)
    ungroup = ungroup_matrix(lens, pack)
    for m in range(3):
        d_flat[m] = dot(ungroup, d_packed[m]).astype(BF16)
    vectors[2:3] = colsum(d_flat[0].astype(F32))
    vectors[3:4] = colsum(d_flat[2].astype(F32))
    d_normed = dot_nt(d_flat[0], matrix[:, blocks_of(0)])
    for m in (1, 2):
        d_normed += dot_nt(d_flat[m], matrix[:, blocks_of(m)])
    normed, inverse = normalize(x[...].astype(F32))
    vectors[0:1] = colsum(d_normed * normed)
    vectors[1:2] = colsum(d_normed)
    vectors[6:10] = jnp.zeros((4, D), F32)
    d_x[...] = (g + norm_back(d_normed, row(e, 0), normed, inverse)).astype(BF16)


def encoder_attention_back(lens, which, g, x, matrices, e, state):
    return pl.pallas_call(
        encoder_attention_back_kernel,
        grid=(1,),
        in_specs=[
            SMEM,
            SMEM,
            full((CAP, D)),
            full((CAP, D)),
            slot_of(0, (D, FF)),
            full((6, D)),
            lead(3, (PAD, D)),
            full((IMGS, PAIRS, SLOT, 2 * SLOT)),
            full((CAP, D)),
        ],
        out_specs=(full((CAP, D)), lead(3, (CAP, D)), full((CAP, D)), full((10, D))),
        out_shape=(ROWS, *ATT_GRADS),
        scratch_shapes=[pltpu.VMEM((PAD, D), BF16), pltpu.VMEM((3, PAD, D), BF16)],
        compiler_params=params(),
        name="encoder_attention_back",
    )(lens, which, g, x, matrices, e, state[1], state[2], state[4])


def table_rows(indices, table):
    places = lax.broadcasted_iota(jnp.int32, (indices.shape[0], table.shape[0]), 1)
    chosen = jnp.where(places == indices[...], 1.0, 0.0).astype(BF16)
    values = table[...]
    top = values.astype(BF16)
    values = values - top.astype(F32)
    middle = values.astype(BF16)
    bottom = (values - middle.astype(F32)).astype(BF16)
    return (dot(chosen, top) + dot(chosen, middle)) + dot(chosen, bottom)


def regressor_attention_kernel(
    lens, which, latents, queries, vis, mask, table, matrix, e,
    out, normed, packed, probs, mixed, branch, q_source, k_source, flat, mixed_slots,
):
    pack = which[0]
    residual = queries[...].astype(F32)
    q_source[...] = residual + table_rows(mask, table)
    centred, _ = normalize(q_source[...])
    normed[0] = (centred * row(e, 0) + row(e, 1)).astype(BF16)
    normed[3] = (centred * row(e, 2) + row(e, 3)).astype(BF16)
    centred, _ = normalize(residual)
    normed[4] = (centred * row(e, 4) + row(e, 5)).astype(BF16)
    incoming = latents[...].astype(F32)
    k_source[...] = incoming + table_rows(vis, table)
    centred, _ = normalize(k_source[...])
    normed[1] = (centred * row(e, 2) + row(e, 3)).astype(BF16)
    centred, _ = normalize(incoming)
    normed[2] = (centred * row(e, 4) + row(e, 5)).astype(BF16)
    flat[0] = ((dot(normed[0], matrix[:, blocks_of(0)]) + row(e, 6)).astype(BF16) * 0.125).astype(BF16)
    for m in (1, 3):
        flat[m] = dot(normed[m], matrix[:, blocks_of(1)]).astype(BF16)
    for m in (2, 4):
        flat[m] = (dot(normed[m], matrix[:, blocks_of(2)]) + row(e, 7)).astype(BF16)
    regroup = regroup_matrix(lens, pack)
    for m in range(5):
        packed[m] = dot(regroup, flat[m]).astype(BF16)
    attend(lens, pack, packed, probs, mixed_slots, 2)
    mixed[...] = dot(ungroup_matrix(lens, pack), mixed_slots[...]).astype(BF16)
    total = dot_nt(mixed[...], matrix[:, blocks_of(3)]) + row(e, 8)
    branch[...] = total.astype(BF16)
    out[...] = (residual + row(e, 9) * total).astype(BF16)


def regressor_attention(lens, which, latents, queries, vis, mask, table, matrices, e):
    return pl.pallas_call(
        regressor_attention_kernel,
        grid=(1,),
        in_specs=[
            SMEM,
            SMEM,
            full((CAP, D)),
            full((CAP, D)),
            full((CAP, 1)),
            full((CAP, 1)),
            full(table.shape),
            slot_of(0, (D, FF)),
            full((10, D)),
        ],
        out_specs=(
            full((CAP, D)),
            lead(5, (CAP, D)),
            lead(5, (PAD, D)),
            full((IMGS, PAIRS, SLOT, 4 * SLOT)),
            full((CAP, D)),
            full((CAP, D)),
            full((CAP, D)),
            full((CAP, D)),
        ),
        out_shape=(ROWS, *ATT_STATE),
        scratch_shapes=[pltpu.VMEM((5, CAP, D), BF16), pltpu.VMEM((PAD, D), BF16)],
        compiler_params=params(),
        name="regressor_attention",
    )(lens, which, latents, queries, vis, mask, table, matrices, e)


def regressor_attention_back_kernel(
    lens, which, g_in, latents, queries, q_source, k_source, matrix, e, packed, probs, branch,
    d_latents, d_queries, d_flat, d_branch, vectors, d_slots, d_packed,
):
    pack = which[0]
    g = g_in[...].astype(F32)
    vectors[9:10] = colsum(g * branch[...].astype(F32))
    d_branch[...] = (g * row(e, 9)).astype(BF16)
    vectors[8:9] = colsum(d_branch[...].astype(F32))
    d_mixed = dot(d_branch[...], matrix[:, blocks_of(3)]).astype(BF16)
    d_slots[...] = dot(regroup_matrix(lens, pack), d_mixed).astype(BF16)
    attend_back(packed, probs, d_slots, d_packed, 2)
    ungroup = ungroup_matrix(lens, pack)
    for m in range(5):
        d_flat[m] = dot(ungroup, d_packed[m]).astype(BF16)
    vectors[6:7] = colsum(d_flat[0].astype(F32))
    vectors[7:8] = colsum(d_flat[2].astype(F32)) + colsum(d_flat[4].astype(F32))
    normed, inverse = normalize(q_source[...])
    grad = dot_nt(d_flat[0], matrix[:, blocks_of(0)])
    vectors[0:1] = colsum(grad * normed)
    vectors[1:2] = colsum(grad)
    total = g + norm_back(grad, row(e, 0), normed, inverse)
    grad = dot_nt(d_flat[3], matrix[:, blocks_of(1)])
    k_gain = colsum(grad * normed)
    k_offset = colsum(grad)
    total += norm_back(grad, row(e, 2), normed, inverse)
    normed, inverse = normalize(queries[...].astype(F32))
    grad = dot_nt(d_flat[4], matrix[:, blocks_of(2)])
    v_gain = colsum(grad * normed)
    v_offset = colsum(grad)
    total += norm_back(grad, row(e, 4), normed, inverse)
    d_queries[...] = total.astype(BF16)
    normed, inverse = normalize(k_source[...])
    grad = dot_nt(d_flat[1], matrix[:, blocks_of(1)])
    vectors[2:3] = k_gain + colsum(grad * normed)
    vectors[3:4] = k_offset + colsum(grad)
    total = norm_back(grad, row(e, 2), normed, inverse)
    normed, inverse = normalize(latents[...].astype(F32))
    grad = dot_nt(d_flat[2], matrix[:, blocks_of(2)])
    vectors[4:5] = v_gain + colsum(grad * normed)
    vectors[5:6] = v_offset + colsum(grad)
    total += norm_back(grad, row(e, 4), normed, inverse)
    d_latents[...] = total.astype(BF16)


def regressor_attention_back(lens, which, g, latents, queries, matrices, e, state):
    return pl.pallas_call(
        regressor_attention_back_kernel,
        grid=(1,),
        in_specs=[
            SMEM,
            SMEM,
            full((CAP, D)),
            full((CAP, D)),
            full((CAP, D)),
            full((CAP, D)),
            full((CAP, D)),
            slot_of(0, (D, FF)),
            full((10, D)),
            lead(5, (PAD, D)),
            full((IMGS, PAIRS, SLOT, 4 * SLOT)),
            full((CAP, D)),
        ],
        out_specs=(
            full((CAP, D)),
            full((CAP, D)),
            lead(5, (CAP, D)),
            full((CAP, D)),
            full((10, D)),
        ),
        out_shape=(ROWS, ROWS, *ATT_GRADS),
        scratch_shapes=[pltpu.VMEM((PAD, D), BF16), pltpu.VMEM((5, PAD, D), BF16)],
        compiler_params=params(),
        name="regressor_attention_back",
    )(lens, which, g, latents, queries, state[5], state[6], matrices, e, state[1], state[2], state[4])


def feed_forward_kernel(x, up, down, r, c, out, normed, active, slope, branch, total):
    step = pl.program_id(0)

    @pl.when(step == 0)
    def _():
        centred, _ = normalize(x[...].astype(F32))
        normed[...] = (centred * row(r, 0) + row(r, 1)).astype(BF16)
        total[...] = jnp.zeros_like(total)

    value, steep = gelu_parts(dot(normed[...], up[...]) + c[...])
    active[...] = value.astype(BF16)
    slope[...] = steep.astype(BF16)
    total[...] += dot(active[...], down[...])

    @pl.when(step == pl.num_programs(0) - 1)
    def _():
        summed = total[...] + row(r, 2)
        branch[...] = summed.astype(BF16)
        out[...] = (x[...].astype(F32) + row(r, 3) * summed).astype(BF16)


HIDDEN = pl.BlockSpec((CAP, HB), lambda i: (0, i))
UP = pl.BlockSpec((None, D, HB), lambda i: (1, 0, i))
DOWN = pl.BlockSpec((HB, D), lambda i: (i, 0))
OFFSET = pl.BlockSpec((1, HB), lambda i: (0, i))


def feed_forward(x, matrices, down, r, c):
    return pl.pallas_call(
        feed_forward_kernel,
        grid=(FF // HB,),
        in_specs=[full((CAP, D)), UP, DOWN, full((4, D)), OFFSET],
        out_specs=(full((CAP, D)), full((CAP, D)), HIDDEN, HIDDEN, full((CAP, D))),
        out_shape=(ROWS, *FFN_STATE),
        scratch_shapes=[pltpu.VMEM((CAP, D), F32)],
        compiler_params=params(),
        name="feed_forward",
    )(x, matrices, down, r, c)


def feed_forward_back_kernel(
    several, *refs
):
    g_refs, (x, branch, slope, up, down, r, d_x, d_hidden, d_branch, vectors, d_offset, g, total) = (
        refs[:several],
        refs[several:],
    )
    step = pl.program_id(0)

    @pl.when(step == 0)
    def _():
        g[...] = g_refs[0][...].astype(F32)
        for more in g_refs[1:]:
            g[...] += more[...].astype(F32)
        d_branch[...] = (g[...] * row(r, 3)).astype(BF16)
        vectors[2:3] = colsum(d_branch[...].astype(F32))
        vectors[3:4] = colsum(g[...] * branch[...].astype(F32))
        total[...] = jnp.zeros_like(total)

    d_active = dot_nt(d_branch[...], down[...])
    d_hidden[...] = (d_active * slope[...].astype(F32)).astype(BF16)
    d_offset[...] = colsum(d_hidden[...].astype(F32))
    total[...] += dot_nt(d_hidden[...], up[...])

    @pl.when(step == pl.num_programs(0) - 1)
    def _():
        d_normed = total[...]
        normed, inverse = normalize(x[...].astype(F32))
        vectors[0:1] = colsum(d_normed * normed)
        vectors[1:2] = colsum(d_normed)
        d_x[...] = (g[...] + norm_back(d_normed, row(r, 0), normed, inverse)).astype(BF16)


def feed_forward_back(g, x, state, matrices, down, r):
    return pl.pallas_call(
        functools.partial(feed_forward_back_kernel, len(g)),
        grid=(FF // HB,),
        in_specs=[full((CAP, D)) for _ in g]
        + [full((CAP, D)), full((CAP, D)), HIDDEN, UP, DOWN, full((4, D))],
        out_specs=(full((CAP, D)), HIDDEN, full((CAP, D)), full((4, D)), OFFSET),
        out_shape=(ROWS, *FFN_GRADS),
        scratch_shapes=[pltpu.VMEM((CAP, D), F32), pltpu.VMEM((CAP, D), F32)],
        compiler_params=params(),
        name="feed_forward_back",
    )(*g, x, state[3], state[2], matrices, down, r)


BLOCKS = FF // D
SHARE = BLOCKS + BLOCKS // 2


def weight_grads_kernel(parts, n1, n2, p1, p2, m1, m2, b1, b2, k1, k2, h1, h2, a1, a2, c1, c2, out):
    step = pl.program_id(0)

    @pl.when(step < 3)
    def _():
        place = 0 if parts == 1 else step
        total = dot_tn(n1[place], p1[step]) + dot_tn(n2[place], p2[step])
        out[...] = total.astype(BF16)
        if parts == 2:

            @pl.when(step > 0)
            def _():
                more = dot_tn(n1[step + 2], p1[step + 2]) + dot_tn(n2[step + 2], p2[step + 2])
                out[...] = (total + more).astype(BF16)

    @pl.when(step == 3)
    def _():
        out[...] = (dot_tn(b1[...], m1[...]) + dot_tn(b2[...], m2[...])).astype(BF16)

    @pl.when((step >= 4) & (step < 8))
    def _():
        out[...] = (dot_tn(k1[...], h1[...]) + dot_tn(k2[...], h2[...])).astype(BF16)

    @pl.when(step >= 8)
    def _():
        out[...] = (dot_tn(a1[...], c1[...]) + dot_tn(a2[...], c2[...])).astype(BF16)


def grad_place(step):
    tail = jnp.maximum(step - 2 * BLOCKS, 0)
    late = jnp.where(step >= 2 * BLOCKS, 1, 0)
    section = (1 - late) * (step // BLOCKS) + late * (tail // 2)
    block = (1 - late) * (step % BLOCKS) + late * (BLOCKS + tail % 2)
    return section, block, 0, 0


def weight_grads(parts, kept, grads):
    att, ffn = [k[2] for k in kept], [k[3] for k in kept]
    att_grads, ffn_grads = [g[2] for g in grads], [g[3] for g in grads]
    have = 1 if parts == 1 else 5
    made = 3 if parts == 1 else 5
    rows = full((CAP, D))
    up_part = pl.BlockSpec((CAP, D), lambda i: (0, jnp.clip(i - BLOCKS, 0, BLOCKS - 1)))
    down_part = pl.BlockSpec((CAP, D), lambda i: (0, jnp.clip(i - 2 * BLOCKS, 0, BLOCKS - 1)))
    return pl.pallas_call(
        functools.partial(weight_grads_kernel, parts),
        grid=(3 * BLOCKS,),
        in_specs=[lead(have, (CAP, D))] * 2
        + [lead(made, (CAP, D))] * 2
        + [rows] * 6
        + [up_part] * 2
        + [down_part] * 2
        + [rows] * 2,
        out_specs=pl.BlockSpec((None, None, D, D), grad_place),
        out_shape=sds((2, SHARE, D, D), BF16),
        compiler_params=params(),
        name="weight_grads",
    )(
        att[0][0], att[1][0], att_grads[0][0], att_grads[1][0],
        att[0][3], att[1][3], att_grads[0][1], att_grads[1][1],
        ffn[0][0], ffn[1][0], ffn_grads[0][0], ffn_grads[1][0],
        ffn[0][1], ffn[1][1], ffn_grads[0][1], ffn_grads[1][1],
    )


MESH = pl.DeviceIdType.MESH


def gather_weights_kernel(matrix, down, matrices, downs, send, receive, local):
    dp, section = lax.axis_index("dp"), lax.axis_index("section")
    odd = lax.rem(section, 2)
    partner = (dp, section + 1 - 2 * odd)
    barrier = pltpu.get_barrier_semaphore()
    pl.semaphore_signal(barrier, inc=1, device_id=partner, device_id_type=MESH)
    pl.semaphore_wait(barrier, 1)
    half = down.shape[0]
    places = (
        (matrix.at[0], matrices.at[odd]),
        (down, downs.at[pl.ds(pl.multiple_of(odd * half, half), half)]),
    )
    copies = []
    for i, (source, target) in enumerate(places):
        away = pltpu.make_async_remote_copy(
            source, target, send.at[i], receive.at[i], device_id=partner, device_id_type=MESH
        )
        away.start()
        here = pltpu.make_async_copy(source, target, local.at[i])
        here.start()
        copies += [away, here]
    for copy in copies:
        copy.wait()


def gather_weights(matrix, down):
    vmem = pl.BlockSpec(memory_space=pltpu.VMEM)
    return pl.pallas_call(
        gather_weights_kernel,
        in_specs=[vmem, vmem],
        out_specs=(ANY, ANY),
        out_shape=(
            sds((2, *matrix.shape[1:]), matrix.dtype),
            sds((2 * down.shape[0], down.shape[1]), down.dtype),
        ),
        scratch_shapes=[pltpu.SemaphoreType.DMA((2,)) for _ in range(3)],
        compiler_params=params(collective_id=1, has_side_effects=True),
        name="gather_weights",
    )(matrix, down)


RING = 8
SEGMENT = D // RING
PART = SEGMENT // 2
CHAIN = SHARE // 2
VECTORS = 24


def ring_place(d):
    odd = lax.rem(d, 2)
    return (1 - odd) * lax.div(d, 2) + odd * (RING - 1 - lax.div(d, 2))


def ring_device(place):
    place = lax.rem(place + RING, RING)
    late = lax.div(place, RING // 2)
    return (1 - late) * 2 * place + late * (2 * (RING - 1 - place) + 1)


def reduce_kernel(
    grads, swapping, vectors, out_matrix, out_down, swapped, out_vectors,
    mine, partner_part, landing, final, stage, v_sum, v_in,
    pair_send, pair_receive, own_sem, ring_send, ring_receive, last_send, last_receive, out_sem,
    v_send, v_receive, swap_send, swap_receive,
):
    d, section = lax.axis_index("dp"), lax.axis_index("section")
    odd = lax.rem(section, 2)
    place = ring_place(d)
    across = (d, section + 2 - 4 * lax.div(section, 2))
    pair = (d, section + 1 - 2 * odd)
    ways = ((ring_device(place + 1), section), (ring_device(place - 1), section))

    def flipped(bit):
        return d + bit - 2 * bit * lax.rem(lax.div(d, bit), 2)

    levels = (pair, (flipped(1), section), (flipped(2), section), (flipped(4), section), across)
    barrier = pltpu.get_barrier_semaphore()
    for other in (*ways, *levels):
        pl.semaphore_signal(barrier, inc=1, device_id=other, device_id_type=MESH)
    pl.semaphore_wait(barrier, len(ways) + len(levels))

    def rows_of(step, way):
        segment = lax.rem(place + (step if way else -step) + 2 * RING, RING)
        return pl.ds(pl.multiple_of(segment * SEGMENT + way * PART, 8), PART)

    def remote(source, target, send, receive, device):
        return pltpu.make_async_remote_copy(source, target, send, receive, device_id=device, device_id_type=MESH)

    swap = remote(swapping, swapped, swap_send, swap_receive, across)
    swap.start()
    own = pltpu.make_async_copy(grads.at[odd], mine, own_sem)
    own.start()

    def pair_copy(step, way):
        rows = rows_of(step, way)
        return remote(
            grads.at[1 - odd, :, rows, :], partner_part.at[:, rows, :],
            pair_send.at[step, way], pair_receive.at[step, way], pair,
        )

    def start_pair(step, carry):
        for way in range(2):
            pair_copy(step, way).start()
        return carry

    lax.fori_loop(0, RING, start_pair, 0)

    def vector_copy(level):
        return remote(v_sum.at[level], v_in.at[level], v_send.at[level], v_receive.at[level], levels[level])

    def vector_next(level):
        vector_copy(level).wait()
        if level + 1 < len(levels):
            v_sum[level + 1] = v_sum[level] + v_in[level]
            vector_copy(level + 1).start()

    v_sum[0] = vectors[...]
    vector_copy(0).start()

    def blocks(chain):
        return pl.ds(chain * CHAIN, CHAIN)

    def ring_copy(step, way, chain):
        rows = rows_of(step, way)
        return remote(
            mine.at[blocks(chain), rows, :], landing.at[blocks(chain), rows, :],
            ring_send.at[step, way, chain], ring_receive.at[step, way, chain], ways[way],
        )

    def incoming(step, way, chain):
        rows = rows_of(step + 1, way)
        return remote(
            mine.at[blocks(chain), rows, :], landing.at[blocks(chain), rows, :],
            ring_send.at[step, way, chain], ring_receive.at[step, way, chain], ways[way],
        )

    own.wait()
    for way in range(2):
        pair_copy(0, way).wait_recv()
        rows = rows_of(0, way)
        for chain in range(2):
            part = (blocks(chain), rows, slice(None))
            mine[part] = (mine[part].astype(F32) + partner_part[part].astype(F32)).astype(BF16)
            ring_copy(0, way, chain).start()
    vector_next(0)

    def total_of(part):
        return (
            mine[part].astype(F32) + partner_part[part].astype(F32) + landing[part].astype(F32)
        ).astype(BF16)

    def reduce_step(step, carry):
        for chain in range(2):
            for way in range(2):
                if chain == 0:
                    pair_copy(step, way).wait_recv()
                incoming(step - 1, way, chain).wait_recv()
                part = (blocks(chain), rows_of(step, way), slice(None))
                mine[part] = total_of(part)
                ring_copy(step, way, chain).start()
        return carry

    lax.fori_loop(1, RING - 1, reduce_step, 0)
    vector_next(1)

    def last_copy(step, way, chain):
        rows = rows_of(step + RING - 1, way)
        return remote(
            final.at[blocks(chain), rows, :], final.at[blocks(chain), rows, :],
            last_send.at[step, way, chain], last_receive.at[step, way, chain], ways[way],
        )

    def last_incoming(step, way, chain):
        rows = rows_of(step + RING, way)
        return remote(
            final.at[blocks(chain), rows, :], final.at[blocks(chain), rows, :],
            last_send.at[step, way, chain], last_receive.at[step, way, chain], ways[way],
        )

    def out_copies(step, way, chain):
        rows = rows_of(step + RING - 1, way)
        copies = []
        for i in range(CHAIN):
            block = chain * CHAIN + i
            if block < BLOCKS:
                target = out_matrix.at[0, rows, pl.ds(block * D, D)]
            else:
                segment = lax.rem(place + (step + RING - 1 if way else 1 - step - RING) + 4 * RING, RING)
                start = (block - BLOCKS) * D + segment * SEGMENT + way * PART
                target = out_down.at[pl.ds(pl.multiple_of(start, 8), PART), :]
            copies.append(pltpu.make_async_copy(stage.at[way, chain, i], target, out_sem.at[way, chain, i]))
        return copies

    def write_out(step, way, chain, first):
        if not first:
            for copy in out_copies(step - 1, way, chain):
                copy.wait()
        stage[way, chain] = final[blocks(chain), rows_of(step + RING - 1, way), :].astype(F32)
        for copy in out_copies(step, way, chain):
            copy.start()

    for chain in range(2):
        for way in range(2):
            if chain == 0:
                pair_copy(RING - 1, way).wait_recv()
            incoming(RING - 2, way, chain).wait_recv()
            part = (blocks(chain), rows_of(RING - 1, way), slice(None))
            final[part] = total_of(part)
            last_copy(0, way, chain).start()
    vector_next(2)
    for chain in range(2):
        for way in range(2):
            write_out(0, way, chain, True)

    def gather_step(step, carry):
        for chain in range(2):
            for way in range(2):
                last_incoming(step - 1, way, chain).wait_recv()
                last_copy(step, way, chain).start()
                write_out(step, way, chain, False)
        return carry

    lax.fori_loop(1, 3, gather_step, 0)
    vector_next(3)
    lax.fori_loop(3, 5, gather_step, 0)
    vector_next(4)
    out_vectors[0] = v_sum[len(levels) - 1]
    out_vectors[1] = v_in[len(levels) - 1]
    lax.fori_loop(5, RING - 1, gather_step, 0)
    for chain in range(2):
        for way in range(2):
            last_incoming(RING - 2, way, chain).wait_recv()
            write_out(RING - 1, way, chain, False)
    for chain in range(2):
        for way in range(2):
            for copy in out_copies(RING - 1, way, chain):
                copy.wait()

    def all_sent(step, carry):
        for way in range(2):
            for chain in range(2):
                ring_copy(step, way, chain).wait_send()
                last_copy(step, way, chain).wait_send()
        return carry

    lax.fori_loop(0, RING - 1, all_sent, 0)

    def pair_sent(step, carry):
        for way in range(2):
            pair_copy(step, way).wait_send()
        return carry

    lax.fori_loop(0, RING, pair_sent, 0)
    swap.wait()


def reduce_grads(grads, swapping, vectors):
    share = (SHARE, D, D)
    vmem = pl.BlockSpec(memory_space=pltpu.VMEM)
    dma = pltpu.SemaphoreType.DMA
    return pl.pallas_call(
        reduce_kernel,
        in_specs=[ANY, ANY, vmem],
        out_specs=(ANY, ANY, ANY, vmem),
        out_shape=(
            sds((1, D, FF), F32),
            sds((FF // 2, D), F32),
            sds(swapping.shape, swapping.dtype),
            sds((2, VECTORS, D), F32),
        ),
        scratch_shapes=[
            pltpu.VMEM(share, BF16),
            pltpu.VMEM(share, BF16),
            pltpu.VMEM(share, BF16),
            pltpu.VMEM(share, BF16),
            pltpu.VMEM((2, 2, CHAIN, PART, D), F32),
            pltpu.VMEM((5, VECTORS, D), F32),
            pltpu.VMEM((5, VECTORS, D), F32),
            dma((RING, 2)),
            dma((RING, 2)),
            dma,
            dma((RING - 1, 2, 2)),
            dma((RING - 1, 2, 2)),
            dma((RING - 1, 2, 2)),
            dma((RING - 1, 2, 2)),
            dma((2, 2, CHAIN)),
            dma((5,)),
            dma((5,)),
            dma,
            dma,
        ],
        compiler_params=params(56, collective_id=2, has_side_effects=True),
        name="reduce_grads",
    )(grads, swapping, vectors)


def plain_reduce_grads(grads, swapping, vectors):
    odd = lax.rem(lax.axis_index("section"), 2)
    pair = [(0, 1), (1, 0), (2, 3), (3, 2)]
    theirs = lax.dynamic_index_in_dim(grads, 1 - odd, 0, keepdims=False)
    mine = lax.dynamic_index_in_dim(grads, odd, 0, keepdims=False)
    total = lax.psum(mine + lax.ppermute(theirs, "section", pair), "dp").astype(F32)
    vectors = lax.psum(vectors + lax.ppermute(vectors, "section", pair), "dp")
    matrix = jnp.swapaxes(total[:BLOCKS], 0, 1).reshape(1, D, FF)
    return (
        matrix,
        total[BLOCKS:].reshape(FF // 2, D),
        swap_layers(swapping),
        jnp.stack([vectors, swap_layers(vectors)]),
    )


def swap_layers(block):
    return lax.ppermute(block, "section", [(0, 2), (1, 3), (2, 0), (3, 1)])


def to_regressor(block):
    return lax.ppermute(block, "section", [(0, 2), (1, 3)])


def to_encoder(block):
    return lax.ppermute(block, "section", [(2, 0), (3, 1)])


def body(
    vis_embed, latent_cot, reg_queries, out_cot, section_matrix, down_weight, enc_vectors, reg_vectors,
    mlp_vectors, hidden_bias, pos_table, image_lengths, vis_index, mask_index,
):
    section = lax.axis_index("section")
    odd = lax.rem(section, 2)
    is_reg = section >= 2
    layer = jnp.where(is_reg, 1, 0)
    matrices, down = gather_weights(section_matrix, down_weight)
    r = lax.dynamic_index_in_dim(mlp_vectors, layer, 0, keepdims=False)
    c = lax.dynamic_slice_in_dim(hidden_bias, layer, 1, 0)
    packs = [(odd + 2 * i).reshape(1).astype(jnp.int32) for i in range(2)]
    vis = [lax.dynamic_slice_in_dim(vis_index, (odd + 2 * i) * CAP, CAP)[:, None] for i in range(2)]
    mask = [lax.dynamic_slice_in_dim(mask_index, (odd + 2 * i) * CAP, CAP)[:, None] for i in range(2)]

    outgoing = jnp.where(is_reg, jnp.stack([vis_embed, latent_cot]), jnp.stack([reg_queries, out_cot]))
    incoming = swap_layers(outgoing)

    def attention_out(result):
        return result[0], tuple(result[1:])

    def enc_forward(i, x):
        mid, att = attention_out(encoder_attention(image_lengths, packs[i], x, matrices, enc_vectors))
        out, ffn = attention_out(feed_forward(mid, matrices, down, r, c))
        return mid, out, att, ffn

    def reg_forward(i, latents, queries):
        mid, att = attention_out(
            regressor_attention(
                image_lengths, packs[i], latents, queries, vis[i], mask[i], pos_table, matrices, reg_vectors
            )
        )
        out, ffn = attention_out(feed_forward(mid, matrices, down, r, c))
        return mid, out, att, ffn

    def no_forward():
        made = unset((ROWS, ROWS, *ATT_STATE, *FFN_STATE))
        split = 2 + len(ATT_STATE)
        return made[0], made[1], tuple(made[2:split]), tuple(made[split:])

    def enc_back(i, g, x, kept):
        mid, _, att, ffn = kept
        d_mid, *ffn_grads = feed_forward_back(g, mid, ffn, matrices, down, r)
        d_x, *att_grads = encoder_attention_back(image_lengths, packs[i], d_mid, x, matrices, enc_vectors, att)
        return d_x, d_x, tuple(att_grads), tuple(ffn_grads)

    def reg_back(i, g, latents, queries, kept):
        mid, _, att, ffn = kept
        d_mid, *ffn_grads = feed_forward_back(g, mid, ffn, matrices, down, r)
        d_latents, d_queries, *att_grads = regressor_attention_back(
            image_lengths, packs[i], d_mid, latents, queries, matrices, reg_vectors, att
        )
        return d_latents, d_queries, tuple(att_grads), tuple(ffn_grads)

    def no_back():
        made = unset((ROWS, ROWS, *ATT_GRADS, *FFN_GRADS))
        split = 2 + len(ATT_GRADS)
        return made[0], made[1], tuple(made[2:split]), tuple(made[split:])

    x = [vis_embed, incoming[0]]
    lat_cot = [latent_cot, incoming[1]]
    queries = [incoming[0], reg_queries]
    cot = [incoming[1], out_cot]

    first = lax.cond(is_reg, no_forward, lambda: enc_forward(0, x[0]))
    latents1 = to_regressor(first[1])
    second = lax.cond(is_reg, lambda: reg_forward(0, latents1, queries[0]), lambda: enc_forward(1, x[1]))
    latents2 = to_regressor(second[1])
    reg_grads1 = lax.cond(is_reg, lambda: reg_back(0, [cot[0]], latents1, queries[0], second), no_back)
    d_latents1 = to_encoder(reg_grads1[0])
    enc_grads1, third = lax.cond(
        is_reg,
        lambda: (no_back(), reg_forward(1, latents2, queries[1])),
        lambda: (enc_back(0, [lat_cot[0], d_latents1], x[0], first), no_forward()),
    )
    reg_grads2 = lax.cond(is_reg, lambda: reg_back(1, [cot[1]], latents2, queries[1], third), no_back)
    d_latents2 = to_encoder(reg_grads2[0])

    def total_vectors(grads1, grads2):
        att, ffn = grads1[2][2] + grads2[2][2], grads1[3][2] + grads2[3][2]
        offset = (grads1[3][3] + grads2[3][3]).reshape(BLOCKS, D)
        return jnp.concatenate([att, ffn, offset, jnp.zeros((VECTORS - 18, D), F32)])

    def last_reg():
        return (
            *no_back(),
            weight_grads(2, (second, third), (reg_grads1, reg_grads2)),
            total_vectors(reg_grads1, reg_grads2),
            jnp.stack([second[1], reg_grads1[1]]),
        )

    def last_enc():
        grads2 = enc_back(1, [lat_cot[1], d_latents2], x[1], second)
        return (
            *grads2,
            weight_grads(1, (first, second), (enc_grads1, grads2)),
            total_vectors(enc_grads1, grads2),
            jnp.stack([grads2[0], grads2[0]]),
        )

    last = lax.cond(is_reg, last_reg, last_enc)
    grads, vectors, swapping = last[4:]
    reduce = reduce_grads if lax.axis_size("dp") == RING else plain_reduce_grads
    matrix_grad, down_grad, swapped, vectors = reduce(grads, swapping, vectors)

    def pick(reg, enc):
        return jnp.where(is_reg, reg, enc)

    latents = pick(latents2, first[1])
    regressed = pick(third[1], swapped[0])
    vis_grad = pick(swapped[0], enc_grads1[0])
    query_grad = pick(reg_grads2[1], swapped[1])
    enc_total, reg_total = pick(vectors[1], vectors[0]), pick(vectors[0], vectors[1])
    return (
        latents,
        regressed,
        vis_grad,
        query_grad,
        matrix_grad,
        down_grad,
        enc_total[:6],
        reg_total[:10],
        jnp.stack([enc_total[10:14], reg_total[10:14]]),
        jnp.stack([enc_total[14:18].reshape(FF), reg_total[14:18].reshape(FF)]),
    )


def solution(mesh):
    rows = P(("dp", "section"), None)
    in_specs = (
        rows, rows, rows, rows, P("section", None, None), P("section", None),
        P(), P(), P(), P(), P(), P("dp", None), P("dp"), P("dp"),
    )
    out_specs = (rows, rows, rows, rows, P("section", None, None), P("section", None), P(), P(), P(), P())
    return jax.shard_map(body, mesh=mesh, in_specs=in_specs, out_specs=out_specs, check_vma=False)
```

time: 2060 us -> 476 us (0.23)
  waiting for transfers between devices: 702 us -> 101 us
  loops' own time: 365 us -> 17.9 us
  Pallas kernels: 0 us -> 289 us
  local copies, waits for them, and re-layouts: 292 us -> 20.7 us
  other arithmetic: 275 us -> 9.55 us
  matrix products: 229 us -> 0 us
  starting transfers between devices: 126 us -> 29.4 us
  blocking collectives: 51.5 us -> 0 us
    psum x2 -> x0, waiting for transfers between devices: 436 us -> none  [the longest x1 436 us: body(): first_total, down_total = lax.psum((own_first, own_down), 'dp')]
    another operation x16 -> x6, loops' own time: 365 us -> 17.9 us  [the longest x1 16 us: body(): lax.cond(is_reg, lambda: reg_back(1, [cot[1]], latents2, queries[1], thir...]
    pallas_call x0 -> x14, Pallas kernels: none -> 289 us  [the longest x1 147 us: reduce_grads(): pl.pallas_call(reduce_kernel, in_specs=[ANY, ANY, vmem], out_specs=(ANY,...]
    dot_general x56 -> x0, matrix products: 182 us -> none  [the longest x12 40.3 us: project(): return jnp.dot(left_side, right_side, preferred_element_type=jnp.float32)]
    add x42 -> x3, other arithmetic: 153 us -> 1.35 us  [the longest x2 0.72 us: total_vectors(): att, ffn = (grads1[2][2] + grads2[2][2], grads1[3][2] + grads2[3][2])]
    ppermute x16 -> x5, waiting for transfers between devices: 243 us -> 101 us  [the longest x2 79.7 us: to_encoder(): return lax.ppermute(block, 'section', [(2, 0), (3, 1)])]
    ppermute x16 -> x5, starting transfers between devices: 122 us -> 29.4 us  [the longest x2 23.9 us: to_regressor(): return lax.ppermute(block, 'section', [(0, 2), (1, 3)])]
    broadcast_in_dim x56 -> x0, local copies, waits for them, and re-layouts: 58.5 us -> none  [the longest x7 29.8 us: body(): zero_down = jnp.zeros((hidden_width, model_width), jnp.float32)]
  transfers between devices with their start and end apart: 19 -> 5, of which waited for: 6 -> 4; matrix products, arithmetic and copies ran while one was open for 14% -> 1% of each run, Pallas kernels for 0% -> 8%
where the time goes in v1:
time: 476 us; the launch traced here: 469 us
  Pallas kernels  289 us (61%)
  waiting for transfers between devices  101 us (21%)
  starting transfers between devices  29.4 us (6%)
  local copies, waits for them, and re-layouts  20.7 us (4%)
  loops' own time  17.9 us (4%)
  other arithmetic  9.55 us (2%)
    pallas_call x1, Pallas kernels, reduce_grads(): pl.pallas_call(reduce_kernel, in_specs=[ANY, ANY, vmem], out_specs=(ANY,...  147 us
    ppermute x2, waiting for transfers between devices, to_encoder(): return lax.ppermute(block, 'section', [(2, 0), (3, 1)])  79.7 us
    pallas_call x2, Pallas kernels, encoder_attention_back(): pl.pallas_call(encoder_attention_back_kernel, grid=(1,), in_specs=[SMEM,...  33.5 us
    pallas_call x2, Pallas kernels, feed_forward(): pl.pallas_call(feed_forward_kernel, grid=(FF // HB,), in_specs=[full((CAP...  25.2 us
    ppermute x2, starting transfers between devices, to_regressor(): return lax.ppermute(block, 'section', [(0, 2), (1, 3)])  23.9 us
    pallas_call x2, Pallas kernels, encoder_attention(): pl.pallas_call(encoder_attention_kernel, grid=(1,), in_specs=[SMEM, SMEM,...  23.6 us
    pallas_call x2, Pallas kernels, feed_forward_back(): pl.pallas_call(functools.partial(feed_forward_back_kernel, len(g)), grid=...  23.3 us
    pallas_call x1, Pallas kernels, weight_grads(): pl.pallas_call(functools.partial(weight_grads_kernel, parts), grid=(3 * B...  22.7 us
  transfers between devices with their start and end apart: 5, of which 4 were waited for; matrix products, arithmetic and copies ran while one was open for 1% of the time, Pallas kernels for 8%

profile of v1, /device:TPU:0, one launch (start us, length us, event | category | flops | bytes accessed | tf_op | source)
XLA Modules:
  0.0 469.3 jit_solution(5441534172151572617)
XLA Ops:
  0.7 3.0 maximum_select_fusion
  3.6 2.9 collective-permute-start
  6.6 13.9 %gather_weights.1 = (bf16[2,768,3072]{2,1,0:T(8,128)(2,1)}, bf16[3072,768]{1,0:T(8,128)(2,1)}) custom-call(bf16[1,768,3072]{2,1,0:T(8,128)(2,1)} %matrix.1, bf16[1536,768]{1,0:T(8,128)(2,1)S(1)} %copy-done.3), custom_call_target="tpu_custom_call" | custom-call | tf_op jit(solution)/shard_map/gather_weights/pallas_call | solution.py:683
  21.1 24.0 %conditional.6 = (bf16[384,768]{1,0:T(8,128)(2,1)}, bf16[384,768]{1,0:T(8,128)(2,1)S(1)}, bf16[5,384,768]{2,1,0:T(8,128)(2,1)}, bf16[5,512,768]{2,1,0:T(8,128)(2...) conditional(s32[]{:T(128)} %convert_element_type.2, ...), branch_computations={%region_0.1_spmd, %region_1.2_spmd} | conditional | bytes 2359412 | solution.py:1044
  21.2 11.3 %encoder_attention.2 = (bf16[384,768]{1,0:T(8,128)(2,1)S(1)}, bf16[5,384,768]{2,1,0:T(8,128)(2,1)}, bf16[5,512,768]{2,1,0:T(8,128)(2,1)}, bf16[4,6,128,512]{3,2,...) custom-call(s32[4,4]{1,0:T(4,128)S(1)} %get-tuple-element.286.lens, ...), custom_call_target="tpu_custom_call" | custom-call | tf_op jit(solution)/shard_map/cond/branch_0_fun/encoder_attention/pallas_call | solution.py:274
  32.5 12.6 %feed_forward.4 = (bf16[384,768]{1,0:T(8,128)(2,1)S(1)}, bf16[384,768]{1,0:T(8,128)(2,1)}, bf16[384,3072]{1,0:T(8,128)(2,1)}, bf16[384,3072]{1,0:T(8,128)(2,1)}, bf16[384,768]{1,0:T(8,128)(2,1)}) custom-call(bf16[384,768]{1,0:T(8,128)(2,1)S(1)} %get-tuple-element.817.x, bf16[2,768,3072]{2,1,0:T(8,128)(2,1)} %get-tuple-element.289.matrix.up, ...), custom_call_target="tpu_custom_call" | custom-call | tf_op jit(solution)/shard_map/cond/branch_0_fun/feed_forward/pallas_call | solution.py:525
  48.8 11.0 %collective-permute-done.1 = bf16[384,768]{1,0:T(8,128)(2,1)S(1)} collective-permute-done((bf16[384,768]{1,0:T(8,128)(2,1)S(1)}, bf16[384,768]{1,0:T(8,128)(2,1)S(1)}, u32[]{:S(2)}, u32[]{:S(2)}) %collective-permute-start.1) | collective-permute-done | bytes 589856 | tf_op jit(solution)/shard_map/ppermute | solution.py:973
  60.5 25.2 %conditional.7 = (bf16[384,768]{1,0:T(8,128)(2,1)}, bf16[384,768]{1,0:T(8,128)(2,1)}, bf16[5,384,768]{2,1,0:T(8,128)(2,1)}, bf16[5,512,768]{2,1,0:T(8,128)(2,1)}...) conditional(s32[]{:T(128)} %convert_element_type.2, ...), branch_computations={%region_2.3_spmd, %region_3.4_spmd.clone} | conditional | bytes 12400 | solution.py:1046
  60.7 12.3 %encoder_attention.3 = (bf16[384,768]{1,0:T(8,128)(2,1)}, bf16[5,384,768]{2,1,0:T(8,128)(2,1)}, bf16[5,512,768]{2,1,0:T(8,128)(2,1)}, bf16[4,6,128,512]{3,2,1,0:...) custom-call(s32[4,4]{1,0:T(4,128)S(1)} %get-tuple-element.316.lens, ...), custom_call_target="tpu_custom_call" | custom-call | tf_op jit(solution)/shard_map/cond/branch_0_fun/encoder_attention/pallas_call | solution.py:274
  73.0 12.5 %feed_forward.5 = (bf16[384,768]{1,0:T(8,128)(2,1)}, bf16[384,768]{1,0:T(8,128)(2,1)}, bf16[384,3072]{1,0:T(8,128)(2,1)}, bf16[384,3072]{1,0:T(8,128)(2,1)S(1)}, bf16[384,768]{1,0:T(8,128)(2,1)}) custom-call(bf16[384,768]{1,0:T(8,128)(2,1)} %get-tuple-element.839.x, bf16[2,768,3072]{2,1,0:T(8,128)(2,1)} %get-tuple-element.319.matrix.up, ...), custom_call_target="tpu_custom_call" | custom-call | tf_op jit(solution)/shard_map/cond/branch_0_fun/feed_forward/pallas_call | solution.py:525
  85.8 22.5 %collective-permute-start.2 = (bf16[384,768]{1,0:T(8,128)(2,1)}, bf16[384,768]{1,0:T(8,128)(2,1)S(1)}, u32[]{:S(2)}, u32[]{:S(2)}) collective-permute-start(bf16[384,768]{1,0:T(8,128)(2,1)} %get-tuple-element.634), channel_id=1, source_target_pairs={{0,2},{1,3},{4,6},{5,7},{8,10},{9,11},{12,14},{13,15},{16,18},{17,... | collective-permute-start | bytes 1769480 | tf_op jit(solution)/shard_map/ppermute | solution.py:973
  110.1 10.8 %collective-permute-done.2 = bf16[384,768]{1,0:T(8,128)(2,1)S(1)} collective-permute-done((bf16[384,768]{1,0:T(8,128)(2,1)}, bf16[384,768]{1,0:T(8,128)(2,1)S(1)}, u32[]{:S(2)}, u32[]{:S(2)}) %collective-permute-start.2) | collective-permute-done | bytes 589856 | tf_op jit(solution)/shard_map/ppermute | solution.py:973
  120.9 35.8 %collective-permute-done.3 = bf16[384,768]{1,0:T(8,128)(2,1)S(1)} collective-permute-done((bf16[384,768]{1,0:T(8,128)(2,1)}, bf16[384,768]{1,0:T(8,128)(2,1)S(1)}, u32[]{:S(2)}, u32[]{:S(2)}) %collective-permute-start.3) | collective-permute-done | bytes 589856 | tf_op jit(solution)/shard_map/ppermute | solution.py:977
  156.7 29.9 %conditional.9 = (bf16[384,768]{1,0:T(8,128)(2,1)}, bf16[5,384,768]{2,1,0:T(8,128)(2,1)}, bf16[384,768]{1,0:T(8,128)(2,1)}, f32[10,768]{1,0:T(8,128)}, bf16[384,...) conditional(s32[]{:T(128)} %convert_element_type.2, ...), branch_computations={%region_6.7_spmd, %region_7.8_spmd.clone} | conditional | bytes 4792572 | solution.py:1050
  156.9 12.3 %feed_forward_back.5 = (bf16[384,768]{1,0:T(8,128)(2,1)S(1)}, bf16[384,3072]{1,0:T(8,128)(2,1)}, bf16[384,768]{1,0:T(8,128)(2,1)}, f32[4,768]{1,0:T(4,128)}, f32[1,3072]{1,0:T(1,128)}) custom-call(bf16[384,768]{1,0:T(8,128)(2,1)} %get-tuple-element.391.refs_0_, bf16[384,768]{1,0:T(8,128)(2,1)S(1)} %get-tuple-element.392.refs_1_, ...), custom_call_target="tpu_custom_call" | custom-call | tf_op jit(solution)/shard_map/cond/branch_0_fun/feed_forward_back/pallas_call | solution.py:571
  169.2 17.0 %encoder_attention_back.2 = (bf16[384,768]{1,0:T(8,128)(2,1)}, bf16[5,384,768]{2,1,0:T(8,128)(2,1)}, bf16[384,768]{1,0:T(8,128)(2,1)}, f32[10,768]{1,0:T(8,128)}) custom-call(s32[4,4]{1,0:T(4,128)S(1)} %get-tuple-element.389.lens, s32[1]{0:T(128)} %get-tuple-element.390.which, bf16[384,768]{1,0:T(8,128)(2,1)S(1)} %get-tuple-element.399.g_in, ...), custom_call_target="tpu_custom_call" | custom-call | tf_op jit(solution)/shard_map/cond/branch_0_fun/encoder_attention_back/pallas_call | solution.py:322
  186.7 16.0 %conditional.10 = ((bf16[384,768]{1,0:T(8,128)(2,1)}, bf16[384,768]{1,0:T(8,128)(2,1)}, bf16[5,384,768]{2,1,0:T(8,128)(2,1)}, bf16[384,768]{1,0:T(8,128)(2,1)}, ...) conditional(s32[]{:T(128)} %convert_element_type.2, () %tuple.62, ...), branch_computations={%region_8.9_spmd, %region_9.10_spmd} | conditional | bytes 42590484 | solution.py:1055
  204.0 43.9 %collective-permute-done.4 = bf16[384,768]{1,0:T(8,128)(2,1)S(1)} collective-permute-done((bf16[384,768]{1,0:T(8,128)(2,1)}, bf16[384,768]{1,0:T(8,128)(2,1)S(1)}, u32[]{:S(2)}, u32[]{:S(2)}) %collective-permute-start.4) | collective-permute-done | bytes 589856 | tf_op jit(solution)/shard_map/ppermute | solution.py:977
  247.9 56.9 %conditional.11 = (bf16[2,6,768,768]{3,2,1,0:T(8,128)(2,1)}, f32[24,768]{1,0:T(8,128)S(1)}, bf16[2,384,768]{2,1,0:T(8,128)(2,1)S(1)}) conditional(s32[]{:T(128)} %convert_element_type.2, (bf16[384,768]{1,0:T(8,128)(2,1)}, bf16[384,768]{1,0:T(8,128)(2,1)S(1)}, bf16[384,768]{1,0:T(8,128)(2,1)}, bf16[384,768]{1,0:T(8,128)(2,1)}, ...), branch_computations={%region_10.11_spmd, %region_11.12_spmd} | conditional | flops 658944 | bytes 58983392 | solution.py:1080
  249.9 11.0 %feed_forward_back.7 = (bf16[384,768]{1,0:T(8,128)(2,1)S(1)}, bf16[384,3072]{1,0:T(8,128)(2,1)S(1)}, bf16[384,768]{1,0:T(8,128)(2,1)S(1)}, f32[4,768]{1,0:T(4,128)S(1)}, f32[1,3072]{1,0:T(1,128)S(1)}) custom-call(bf16[384,768]{1,0:T(8,128)(2,1)} %get-tuple-element.491.refs_0_, bf16[384,768]{1,0:T(8,128)(2,1)S(1)} %get-tuple-element.492.refs_1_, ...), custom_call_target="tpu_custom_call" | custom-call | tf_op jit(solution)/shard_map/cond/branch_0_fun/feed_forward_back/pallas_call | solution.py:571
  263.7 16.4 %encoder_attention_back.3 = (bf16[384,768]{1,0:T(8,128)(2,1)S(1)}, bf16[5,384,768]{2,1,0:T(8,128)(2,1)S(1)}, bf16[384,768]{1,0:T(8,128)(2,1)S(1)}, f32[10,768]{1,0:T(8,128)S(1)}) custom-call(s32[4,4]{1,0:T(4,128)S(1)} %get-tuple-element.489.lens, s32[1]{0:T(128)} %get-tuple-element.490.which, bf16[384,768]{1,0:T(8,128)(2,1)S(1)} %get-tuple-element.499.g_in, ...), custom_call_target="tpu_custom_call" | custom-call | tf_op jit(solution)/shard_map/cond/branch_0_fun/encoder_attention_back/pallas_call | solution.py:322
  281.8 22.7 %weight_grads.2 = bf16[2,6,768,768]{3,2,1,0:T(8,128)(2,1)} custom-call(bf16[5,384,768]{2,1,0:T(8,128)(2,1)} %get-tuple-element.486.n1, bf16[5,384,768]{2,1,0:T(8,128)(2,1)} %get-tuple-element.487.n2, bf16[5,384,768]{2,1,0:T(8,128)(2,1)S(1)} %copy-done.13, bf16[5,384,768]{2,1,0:T(8,128)(2,1)} %copy-done.2, bf16[384,768]{1,0:T(8,128)(2,1)} %get-tuple-element.506.m1, ...), custom_call_target="tpu_custom_call" | custom-call | tf_op jit(solution)/shard_map/cond/branch_0_fun/weight_grads/pallas_call | solution.py:632
  304.8 146.9 %reduce_grads.1 = (f32[1,768,3072]{2,1,0:T(8,128)}, f32[1536,768]{1,0:T(8,128)}, bf16[2,384,768]{2,1,0:T(8,128)(2,1)}, f32[2,24,768]{2,1,0:T(8,128)}) custom-call(bf16[2,6,768,768]{3,2,1,0:T(8,128)(2,1)} %get-tuple-element.694.grads, bf16[2,384,768]{2,1,0:T(8,128)(2,1)S(1)} %get-tuple-element.695.swapping, f32[24,768]{1,0:T(8,128)S(1)} %get-tuple-element.696.vectors), custom_call_target="tpu_custom_call" | custom-call | tf_op jit(solution)/shard_map/reduce_grads/pallas_call | solution.py:916
  458.1 8.7 %copy.164 = f32[1,768,3072]{2,1,0:T(8,128)} copy(f32[1,768,3072]{2,1,0:T(8,128)} %get-tuple-element.963) | data formatting | bytes 18874368
  (98 shorter events, 23.2 us)
Async XLA Ops:
  0.6 19.8 %copy-start = (f32[2,4,768]{2,1,0:T(4,128)S(1)}, f32[2,4,768]{2,1,0:T(4,128)}, u32[]{:S(2)}) copy-start(f32[2,4,768]{2,1,0:T(4,128)} %param.34) | copy-start | bytes 73732
  3.6 43.0 %collective-permute-start = (bf16[2,384,768]{2,1,0:T(8,128)(2,1)}, bf16[2,384,768]{2,1,0:T(8,128)(2,1)}, u32[]{:S(2)}, u32[]{:S(2)}) collective-permute-start(bf16[2,384,768]{2,1,0:T(8,128)(2,1)} %maximum_select_fusion), channel_id=1, source_target_pairs={{0,2},{1,3},{2,0},{3,1},{4,6},{5,7},{6,4},{7,5},{8,10},{9,11},{10,... | collective-permute-start | bytes 3538952 | tf_op jit(solution)/shard_map/ppermute | solution.py:969
  6.6 14.6 %copy-start.8 = (bf16[384,768]{1,0:T(8,128)(2,1)S(1)}, bf16[384,768]{1,0:T(8,128)(2,1)}, u32[]{:S(2)}) copy-start(bf16[384,768]{1,0:T(8,128)(2,1)} %param.26) | copy-start | bytes 1769476
  6.6 14.6 %copy-start.35 = (f32[6,768]{1,0:T(8,128)S(1)}, f32[6,768]{1,0:T(8,128)}, u32[]{:S(2)}) copy-start(f32[6,768]{1,0:T(8,128)} %param.32) | copy-start | bytes 55300
  45.1 14.6 %copy-start.33 = (bf16[384,768]{1,0:T(8,128)(2,1)}, bf16[384,768]{1,0:T(8,128)(2,1)S(1)}, u32[]{:S(2)}) copy-start(bf16[384,768]{1,0:T(8,128)(2,1)S(1)} %get-tuple-element.633) | copy-start | bytes 1769476
  45.2 14.6 %copy-start.36 = (f32[6,768]{1,0:T(8,128)S(1)}, f32[6,768]{1,0:T(8,128)}, u32[]{:S(2)}) copy-start(f32[6,768]{1,0:T(8,128)} %param.32) | copy-start | bytes 55300
  45.2 14.6 %collective-permute-start.1 = (bf16[384,768]{1,0:T(8,128)(2,1)S(1)}, bf16[384,768]{1,0:T(8,128)(2,1)S(1)}, u32[]{:S(2)}, u32[]{:S(2)}) collective-permute-start(bf16[384,768]{1,0:T(8,128)(2,1)S(1)} %get-tuple-element.633), channel_id=1, source_target_pairs={{0,2},{1,3},{4,6},{5,7},{8,10},{9,11},{12,14},{13,15},{16,18},{17,... | collective-permute-start | bytes 1769480 | tf_op jit(solution)/shard_map/ppermute | solution.py:973
  48.8 59.5 %copy-start.4 = (bf16[384,768]{1,0:T(8,128)(2,1)}, bf16[384,768]{1,0:T(8,128)(2,1)S(1)}, u32[]{:S(2)}) copy-start(bf16[384,768]{1,0:T(8,128)(2,1)S(1)} %get-tuple-element.807) | copy-start | bytes 1769476
  85.8 35.1 %collective-permute-start.2 = (bf16[384,768]{1,0:T(8,128)(2,1)}, bf16[384,768]{1,0:T(8,128)(2,1)S(1)}, u32[]{:S(2)}, u32[]{:S(2)}) collective-permute-start(bf16[384,768]{1,0:T(8,128)(2,1)} %get-tuple-element.634), channel_id=1, source_target_pairs={{0,2},{1,3},{4,6},{5,7},{8,10},{9,11},{12,14},{13,15},{16,18},{17,... | collective-permute-start | bytes 1769480 | tf_op jit(solution)/shard_map/ppermute | solution.py:973
  108.8 47.9 %collective-permute-start.3 = (bf16[384,768]{1,0:T(8,128)(2,1)}, bf16[384,768]{1,0:T(8,128)(2,1)S(1)}, u32[]{:S(2)}, u32[]{:S(2)}) collective-permute-start(bf16[384,768]{1,0:T(8,128)(2,1)} %get-tuple-element.643), channel_id=1, source_target_pairs={{2,0},{3,1},{6,4},{7,5},{10,8},{11,9},{14,12},{15,13},{18,16},{19,... | collective-permute-start | bytes 1769480 | tf_op jit(solution)/shard_map/ppermute | solution.py:977
  120.9 65.8 %copy-start.6 = (bf16[384,768]{1,0:T(8,128)(2,1)}, bf16[384,768]{1,0:T(8,128)(2,1)S(1)}, u32[]{:S(2)}) copy-start(bf16[384,768]{1,0:T(8,128)(2,1)S(1)} %collective-permute-done.2) | copy-start | bytes 1769476
  202.7 45.2 %collective-permute-start.4 = (bf16[384,768]{1,0:T(8,128)(2,1)}, bf16[384,768]{1,0:T(8,128)(2,1)S(1)}, u32[]{:S(2)}, u32[]{:S(2)}) collective-permute-start(bf16[384,768]{1,0:T(8,128)(2,1)} %get-tuple-element.659), channel_id=1, source_target_pairs={{2,0},{3,1},{6,4},{7,5},{10,8},{11,9},{14,12},{15,13},{18,16},{19,... | collective-permute-start | bytes 1769480 | tf_op jit(solution)/shard_map/ppermute | solution.py:977
  263.6 18.1 %copy-start.40 = (f32[10,768]{1,0:T(8,128)S(1)}, f32[10,768]{1,0:T(8,128)}, u32[]{:S(2)}) copy-start(f32[10,768]{1,0:T(8,128)} %get-tuple-element.518) | copy-start | bytes 92164 | tf_op jit(solution)/shard_map/cond
  263.6 18.1 %copy-start.39 = (f32[4,768]{1,0:T(4,128)S(1)}, f32[4,768]{1,0:T(4,128)}, u32[]{:S(2)}) copy-start(f32[4,768]{1,0:T(4,128)} %reshape.42) | copy-start | bytes 36868 | tf_op jit(solution)/shard_map/cond
  263.6 18.1 %copy-start.43 = (f32[24]{0:T(128)S(1)}, f32[24]{0:T(128)}, u32[]{:S(2)}) copy-start(f32[24]{0:T(128)} %pad.5.clone) | copy-start | bytes 292 | tf_op jit(solution)/shard_map/cond
  263.6 18.2 %copy-start.13 = (bf16[5,384,768]{2,1,0:T(8,128)(2,1)S(1)}, bf16[5,384,768]{2,1,0:T(8,128)(2,1)}, u32[]{:S(2)}) copy-start(bf16[5,384,768]{2,1,0:T(8,128)(2,1)} %get-tuple-element.488.p1) | copy-start | bytes 8847364 | tf_op jit(solution)/shard_map/cond
  263.6 18.2 %copy-start.14 = (bf16[384,3072]{1,0:T(8,128)(2,1)S(1)}, bf16[384,3072]{1,0:T(8,128)(2,1)}, u32[]{:S(2)}) copy-start(bf16[384,3072]{1,0:T(8,128)(2,1)} %get-tuple-element.512.h1) | copy-start | bytes 7077892 | tf_op jit(solution)/shard_map/cond
  263.6 18.2 %copy-start.15 = (bf16[384,3072]{1,0:T(8,128)(2,1)S(1)}, bf16[384,3072]{1,0:T(8,128)(2,1)}, u32[]{:S(2)}) copy-start(bf16[384,3072]{1,0:T(8,128)(2,1)} %get-tuple-element.514.a1) | copy-start | bytes 7077892 | tf_op jit(solution)/shard_map/cond
  263.6 18.2 %copy-start.20 = (bf16[384,768]{1,0:T(8,128)(2,1)S(1)}, bf16[384,768]{1,0:T(8,128)(2,1)}, u32[]{:S(2)}) copy-start(bf16[384,768]{1,0:T(8,128)(2,1)} %get-tuple-element.507.m2) | copy-start | bytes 1769476 | tf_op jit(solution)/shard_map/cond
  263.6 18.2 %copy-start.21 = (bf16[384,768]{1,0:T(8,128)(2,1)S(1)}, bf16[384,768]{1,0:T(8,128)(2,1)}, u32[]{:S(2)}) copy-start(bf16[384,768]{1,0:T(8,128)(2,1)} %get-tuple-element.511.k2) | copy-start | bytes 1769476 | tf_op jit(solution)/shard_map/cond
  304.8 150.4 %copy-start.7 = (bf16[384,768]{1,0:T(8,128)(2,1)S(1)}, bf16[384,768]{1,0:T(8,128)(2,1)}, u32[]{:S(2)}) copy-start(bf16[384,768]{1,0:T(8,128)(2,1)} %copy-done.6) | copy-start | bytes 1769476
  304.8 150.4 %copy-start.29 = (bf16[384,768]{1,0:T(8,128)(2,1)S(1)}, bf16[384,768]{1,0:T(8,128)(2,1)}, u32[]{:S(2)}) copy-start(bf16[384,768]{1,0:T(8,128)(2,1)} %get-tuple-element.698) | copy-start | bytes 1769476
  304.8 150.4 %copy-start.30 = (bf16[384,768]{1,0:T(8,128)(2,1)S(1)}, bf16[384,768]{1,0:T(8,128)(2,1)}, u32[]{:S(2)}) copy-start(bf16[384,768]{1,0:T(8,128)(2,1)} %get-tuple-element.650) | copy-start | bytes 1769476
  304.8 150.4 %copy-start.34 = (bf16[384,768]{1,0:T(8,128)(2,1)S(1)}, bf16[384,768]{1,0:T(8,128)(2,1)}, u32[]{:S(2)}) copy-start(bf16[384,768]{1,0:T(8,128)(2,1)} %copy-done.33) | copy-start | bytes 1769476
  (15 other events, 122.6 us)

commit v2 on v1

v2 whole, which is shorter than its diff:
```python
import functools

import jax
import jax.numpy as jnp
from jax import lax
from jax.experimental import pallas as pl
from jax.experimental.pallas import tpu as pltpu
from jax.sharding import PartitionSpec as P

F32 = jnp.float32
BF16 = jnp.bfloat16
CAP = 384
IMGS = 4
SLOT = 128
PAD = IMGS * SLOT
D = 768
FF = 3072
LANES = 128
PAIRS = D // LANES
BLOCKS = FF // D
VECTORS = 24
EPS = 1e-06
MIB = 1 << 20
ANY = pl.BlockSpec(memory_space=pl.ANY)
SMEM = pl.BlockSpec(memory_space=pltpu.SMEM)


def params(limit=48, **more):
    return pltpu.CompilerParams(vmem_limit_bytes=limit * MIB, **more)


def sds(shape, dtype):
    return jax.ShapeDtypeStruct(shape, dtype)


def dot(a, b):
    return jnp.dot(a, b, preferred_element_type=F32)


def dot_nt(a, b):
    return lax.dot_general(a, b, (((1,), (1,)), ((), ())), preferred_element_type=F32)


def dot_tn(a, b):
    return lax.dot_general(a, b, (((0,), (0,)), ((), ())), preferred_element_type=F32)


def row(ref, i):
    return ref[i : i + 1, :]


def colsum(values):
    return jnp.sum(values, axis=0, keepdims=True)


def normalize(values):
    centred = values - jnp.mean(values, axis=-1, keepdims=True)
    spread = jnp.mean(centred * centred, axis=-1, keepdims=True)
    inverse = lax.rsqrt(spread + EPS)
    return centred * inverse, inverse


def norm_back(gradient, gain, normed, inverse):
    scaled = gradient * gain
    level = jnp.mean(scaled, axis=-1, keepdims=True)
    slope = jnp.mean(scaled * normed, axis=-1, keepdims=True)
    return inverse * (scaled - level - normed * slope)


def gelu_parts(t):
    e = jnp.exp(-0.5 * t * t)
    k = 1.0 / (1.0 + (0.3275911 * 0.7071067811865476) * jnp.abs(t))
    poly = k * (
        0.127414796
        + k * (-0.142248368 + k * (0.7107068705 + k * (-0.7265760135 + k * 0.5307027145)))
    )
    tail = poly * e
    phi = jnp.where(t >= 0.0, 1.0 - tail, tail)
    return t * phi, phi + t * (e * 0.3989422804014327)


CHUNK = 64


def over_rows(body, carry=0, chunk=CHUNK):
    def step(i, carry):
        return body(pl.ds(pl.multiple_of(i * chunk, chunk), chunk), carry)

    return lax.fori_loop(0, CAP // chunk, step, carry)


def each_rows(body, chunk=CHUNK):
    def step(rows, carry):
        body(rows)
        return carry

    over_rows(step, 0, chunk)


def zero_row():
    return jnp.zeros((1, D), F32)


def group_matrices(lens, pack, regroup, ungroup):
    def image(j, start):
        size = lens[pack, j]
        slots = pl.ds(pl.multiple_of(j * SLOT, SLOT), SLOT)
        place = lax.broadcasted_iota(jnp.int32, (SLOT, CAP), 0)
        rows = lax.broadcasted_iota(jnp.int32, (SLOT, CAP), 1)
        hit = (place + start == rows) & (place < size)
        regroup[slots, :] = jnp.where(hit, 1.0, 0.0).astype(BF16)
        place = lax.broadcasted_iota(jnp.int32, (CAP, SLOT), 1)
        rows = lax.broadcasted_iota(jnp.int32, (CAP, SLOT), 0)
        hit = (place + start == rows) & (place < size)
        ungroup[:, slots] = jnp.where(hit, 1.0, 0.0).astype(BF16)
        return start + size

    lax.fori_loop(0, IMGS, image, jnp.int32(0))


def lane_halves():
    lane = lax.broadcasted_iota(jnp.int32, (1, LANES), 1)
    first = jnp.where(lane < LANES // 2, 1.0, 0.0)
    return first.astype(BF16), (1.0 - first).astype(BF16)


def both_heads(block, halves):
    return jnp.concatenate([block * halves[0], block * halves[1]], axis=0)


def merge_heads(stacked):
    keys = stacked.shape[0] // 2
    lane = lax.broadcasted_iota(jnp.int32, (keys, LANES), 1)
    return jnp.where(lane < LANES // 2, stacked[:keys], stacked[keys:])


def softmax(scores):
    raised = jnp.exp(scores - jnp.max(scores, axis=0, keepdims=True))
    return (raised * (1.0 / jnp.sum(raised, axis=0, keepdims=True))).astype(BF16)


def keys_of(packed, first, parts, rows, cols, halves):
    return both_heads(
        jnp.concatenate([packed[first + 2 * m, rows, cols] for m in range(parts)], axis=0), halves
    )


def attend(lens, pack, packed, probs, mixed_slots, parts, done):
    halves = lane_halves()
    keys = SLOT * parts

    def image(j, carry):
        rows = pl.ds(pl.multiple_of(j * SLOT, SLOT), SLOT)
        size = lens[pack, j]
        valid = lax.bitwise_and(lax.broadcasted_iota(jnp.int32, (keys, SLOT), 0), SLOT - 1) < size
        for g in range(PAIRS):
            cols = slice(g * LANES, (g + 1) * LANES)
            scores = dot_nt(keys_of(packed, 1, parts, rows, cols, halves), packed[0, rows, cols])
            low = jnp.concatenate(
                [softmax(jnp.where(valid, part, -1e30)) for part in (scores[:keys], scores[keys:])], axis=0
            )
            probs[j, g] = low
            mixed_slots[rows, cols] = dot_tn(low, keys_of(packed, 2, parts, rows, cols, halves)).astype(BF16)
        done(j)
        return carry

    lax.fori_loop(0, IMGS, image, 0)


def attend_back(packed, probs, mixed_slots, d_mixed_slots, d_packed, parts, ready):
    halves = lane_halves()
    keys = SLOT * parts
    less = both_heads(jnp.full((keys, LANES), -1.0, BF16), halves)

    def image(j, carry):
        ready(j)
        rows = pl.ds(pl.multiple_of(j * SLOT, SLOT), SLOT)
        for g in range(PAIRS):
            cols = slice(g * LANES, (g + 1) * LANES)
            d_out = d_mixed_slots[rows, cols]
            centre = (d_out.astype(F32) * mixed_slots[rows, cols].astype(F32)).astype(BF16)
            low = probs[j, g]
            d_prob = dot_nt(
                jnp.concatenate([keys_of(packed, 2, parts, rows, cols, halves), less], axis=1),
                jnp.concatenate([d_out, centre], axis=1),
            )
            d_scores = (low.astype(F32) * d_prob).astype(BF16)
            d_q = dot_tn(d_scores, keys_of(packed, 1, parts, rows, cols, halves)) * 0.125
            d_packed[0, rows, cols] = d_q.astype(BF16)
            q = packed[0, rows, cols]
            zero = jnp.zeros_like(q)
            sides = jnp.concatenate(
                [jnp.concatenate([q, zero], axis=1), jnp.concatenate([zero, d_out], axis=1)], axis=0
            )
            d_kv = dot(jnp.concatenate([d_scores, low], axis=1), sides)
            d_k = merge_heads(d_kv[:, :LANES]).astype(BF16)
            d_v = merge_heads(d_kv[:, LANES:]).astype(BF16)
            for m in range(parts):
                part = slice(m * SLOT, (m + 1) * SLOT)
                d_packed[1 + 2 * m, rows, cols] = d_k[part]
                d_packed[2 + 2 * m, rows, cols] = d_v[part]
        return carry

    lax.fori_loop(0, IMGS, image, 0)


SQUARE = (D, D)
ROWS = sds((CAP, D), BF16)
STATE = (
    sds((5, CAP, D), BF16),
    sds((5, PAD, D), BF16),
    sds((IMGS, PAIRS, 4 * SLOT, SLOT), BF16),
    sds((CAP, D), BF16),
    sds((CAP, D), BF16),
    sds((2, CAP, D), F32),
    sds((CAP, D), BF16),
    sds((CAP, FF), BF16),
    sds((CAP, FF), BF16),
    sds((CAP, D), BF16),
    sds((PAD, D), BF16),
)
GRADS = (
    sds((5, CAP, D), BF16),
    sds((CAP, D), BF16),
    sds((CAP, FF), BF16),
    sds((CAP, D), BF16),
)
TOTALS = sds((VECTORS, D), F32)
FFN_AT = 10
HIDDEN_AT = FFN_AT + 4


def full(shape):
    return pl.BlockSpec(shape, lambda i: (0,) * len(shape))


def lead(count, shape):
    return pl.BlockSpec((count, *shape), lambda i: (0,) * (1 + len(shape)))


VMEM = pl.BlockSpec(memory_space=pltpu.VMEM)


def unset(shapes):
    def kernel(*refs):
        del refs

    return pl.pallas_call(
        kernel, out_shape=shapes, out_specs=tuple(ANY for _ in shapes), name="unset"
    )()


class Copies:
    def __init__(self, semaphores):
        self.semaphores, self.used, self.open = semaphores, 0, []

    def take(self, count=1):
        self.used += count
        return self.used - count

    def start(self, source, target):
        copy = pltpu.make_async_copy(source, target, self.semaphores.at[self.take()])
        copy.start()
        return copy

    def leave(self, source, target):
        self.open.append(self.start(source, target))

    def finish(self):
        for copy in self.open:
            copy.wait()


def columns(i):
    return slice(i * D, (i + 1) * D)


class Weights:
    def __init__(self, copies, weights, held):
        self.copies, self.weights, self.held, self.started = copies, weights, held, {}

    def target(self, i):
        kind, block = divmod(i, BLOCKS)
        held = self.held[kind]
        return held.at[columns(block), :] if kind == 2 else held.at[:, columns(block)]

    def start(self, *order):
        for i in order:
            self.started[i] = self.copies.start(self.weights.at[i], self.target(i))

    def wait(self, *which):
        for i in which:
            self.started[i].wait()


WEIGHT_SCRATCH = [pltpu.VMEM((D, FF), BF16), pltpu.VMEM((D, FF), BF16), pltpu.VMEM((FF, D), BF16)]
ALL_BLOCKS = range(BLOCKS)
UPS = [BLOCKS + i for i in ALL_BLOCKS]
DOWNS = [2 * BLOCKS + i for i in ALL_BLOCKS]


def feed_forward(copies, weights, mid, r, c, out, state, kept):
    normed, active, slope, branch = state

    def norm(rows):
        centred, _ = normalize(mid[rows, :].astype(F32))
        normed[rows, :] = (centred * row(r, 0) + row(r, 1)).astype(BF16)

    each_rows(norm)
    copies.leave(normed, kept[0])
    _, up, down = weights.held
    for i in ALL_BLOCKS:
        weights.wait(BLOCKS + i)
        value, steep = gelu_parts(dot(normed[...], up[:, columns(i)]) + c[:, columns(i)])
        active[:, columns(i)] = value.astype(BF16)
        slope[:, columns(i)] = steep.astype(BF16)
        copies.leave(active.at[:, columns(i)], kept[1].at[:, columns(i)])
        copies.leave(slope.at[:, columns(i)], kept[2].at[:, columns(i)])
    weights.wait(*DOWNS)
    summed = dot(active[...], down[...]) + row(r, 2)
    branch[...] = summed.astype(BF16)
    out[...] = (mid[...].astype(F32) + row(r, 3) * summed).astype(BF16)
    copies.leave(branch, kept[3])


def feed_forward_back(copies, weights, ready, grads, mid, r, refs, totals, kept, residual):
    slope, branch, d_hidden, d_branch, work = refs
    ready("branch")

    def enter(rows, carry):
        g = grads[0][rows, :].astype(F32)
        for more in grads[1:]:
            g += more[rows, :].astype(F32)
        residual[rows, :] = g
        low = (g * row(r, 3)).astype(BF16)
        d_branch[rows, :] = low
        return carry[0] + colsum(low.astype(F32)), carry[1] + colsum(g * branch[rows, :].astype(F32))

    sums = over_rows(enter, (zero_row(), zero_row()))
    totals[FFN_AT + 2 : FFN_AT + 3], totals[FFN_AT + 3 : FFN_AT + 4] = sums
    copies.leave(d_branch, kept[1])
    for i in ALL_BLOCKS:
        weights.wait(2 * BLOCKS + i)
        ready(i)
        d_active = dot_nt(d_branch[...], weights.held[2][columns(i), :])
        d_hidden[:, columns(i)] = (d_active * slope[:, columns(i)].astype(F32)).astype(BF16)
        copies.leave(d_hidden.at[:, columns(i)], kept[0].at[:, columns(i)])
        at = HIDDEN_AT + i
        totals[at : at + 1] = over_rows(
            lambda rows, sums, i=i: sums + colsum(d_hidden[rows, columns(i)].astype(F32)), zero_row()
        )
    weights.wait(*UPS)
    work[...] = dot_nt(d_hidden[...], weights.held[1][...])

    def leave(rows, carry):
        grad = work[rows, :]
        normed, inverse = normalize(mid[rows, :].astype(F32))
        moved = residual[rows, :] + norm_back(grad, row(r, 0), normed, inverse)
        residual[rows, :] = moved.astype(BF16).astype(F32)
        return carry[0] + colsum(grad * normed), carry[1] + colsum(grad)

    totals[FFN_AT : FFN_AT + 1], totals[FFN_AT + 1 : FFN_AT + 2] = over_rows(leave, (zero_row(), zero_row()))


def attention(copies, lens, pack, parts, refs, kept):
    flat, packed, probs, mixed, mixed_slots, regroup, ungroup = refs
    group_matrices(lens, pack, regroup, ungroup)
    for m in range(1 + 2 * parts):
        packed[m] = dot(regroup[...], flat[m]).astype(BF16)
        copies.leave(packed.at[m], kept[1].at[m])
    first = copies.take(IMGS)

    def probs_copy(j):
        target = kept[2].at[j, :, pl.ds(0, 2 * SLOT * parts), :]
        return pltpu.make_async_copy(probs.at[j], target, copies.semaphores.at[first + j])

    attend(lens, pack, packed, probs, mixed_slots, parts, lambda j: probs_copy(j).start())
    copies.leave(mixed_slots, kept[10])
    mixed[...] = dot(ungroup[...], mixed_slots[...]).astype(BF16)
    copies.leave(mixed, kept[3])
    copies.open += [probs_copy(j) for j in range(IMGS)]


def state_scratch(parts):
    rows = pltpu.VMEM((CAP, D), BF16)
    wide = pltpu.VMEM((CAP, FF), BF16)
    count = 1 + 2 * parts
    return [
        *WEIGHT_SCRATCH,
        pltpu.VMEM((count, CAP, D), BF16),
        pltpu.VMEM((PAD, D), BF16),
        pltpu.VMEM((PAD, CAP), BF16),
        pltpu.VMEM((CAP, PAD), BF16),
        pltpu.VMEM((5 if parts == 2 else 1, CAP, D), BF16),
        pltpu.VMEM((count, PAD, D), BF16),
        pltpu.VMEM((IMGS, PAIRS, 2 * SLOT * parts, SLOT), BF16),
        rows,
        rows,
        pltpu.VMEM((2, CAP, D), F32),
        rows,
        wide,
        wide,
        rows,
        pltpu.SemaphoreType.DMA((64,)),
    ]


def encoder_forward_kernel(lens, which, x, e, r, c, given, mid, out, *refs):
    kept, scratch = refs[: len(STATE)], refs[len(STATE) :]
    (
        *held, flat, mixed_slots, regroup, ungroup, normed, packed, probs, mixed, branch, _, f_normed, active,
        slope, f_branch, semaphores,
    ) = scratch
    copies = Copies(semaphores)
    weights = Weights(copies, given, held)
    weights.start(*ALL_BLOCKS, *UPS, *DOWNS)

    def norm(rows):
        centred, _ = normalize(x[rows, :].astype(F32))
        normed[0, rows, :] = (centred * row(e, 0) + row(e, 1)).astype(BF16)

    each_rows(norm)
    copies.leave(normed.at[0], kept[0].at[0])
    weights.wait(0)
    qkvo = weights.held[0]
    flat[0] = ((dot(normed[0], qkvo[:, columns(0)]) + row(e, 2)).astype(BF16) * 0.125).astype(BF16)
    weights.wait(1)
    flat[1] = dot(normed[0], qkvo[:, columns(1)]).astype(BF16)
    weights.wait(2)
    flat[2] = (dot(normed[0], qkvo[:, columns(2)]) + row(e, 3)).astype(BF16)
    attention(copies, lens, which[0], 1, (flat, packed, probs, mixed, mixed_slots, regroup, ungroup), kept)
    weights.wait(3)
    summed = dot_nt(mixed[...], qkvo[:, columns(3)]) + row(e, 4)
    branch[...] = summed.astype(BF16)
    copies.leave(branch, kept[4])
    mid[...] = (x[...].astype(F32) + row(e, 5) * summed).astype(BF16)
    feed_forward(copies, weights, mid, r, c, out, (f_normed, active, slope, f_branch), kept[6:])
    copies.finish()


def encoder_forward(lens, which, x, e, r, c, weights):
    made = pl.pallas_call(
        encoder_forward_kernel,
        in_specs=[SMEM, SMEM, VMEM, VMEM, VMEM, VMEM, ANY],
        out_specs=(VMEM, VMEM, *(ANY for _ in STATE)),
        out_shape=(ROWS, ROWS, *STATE),
        scratch_shapes=state_scratch(1),
        compiler_params=params(56),
        name="encoder_forward",
    )(lens, which, x, e, r, c, weights)
    return made[0], made[1], tuple(made[2:])


def table_rows(indices, table):
    places = lax.broadcasted_iota(jnp.int32, (indices.shape[0], table.shape[0]), 1)
    chosen = jnp.where(places == indices[...], 1.0, 0.0).astype(BF16)
    values = table[...]
    top = values.astype(BF16)
    values = values - top.astype(F32)
    middle = values.astype(BF16)
    bottom = (values - middle.astype(F32)).astype(BF16)
    return (dot(chosen, top) + dot(chosen, middle)) + dot(chosen, bottom)


def regressor_forward_kernel(lens, which, latents, queries, vis, mask, table, e, r, c, given, mid, out, *refs):
    kept, scratch = refs[: len(STATE)], refs[len(STATE) :]
    (
        *held, flat, mixed_slots, regroup, ungroup, normed, packed, probs, mixed, branch, sources, f_normed,
        active, slope, f_branch, semaphores,
    ) = scratch
    copies = Copies(semaphores)
    weights = Weights(copies, given, held)
    weights.start(*ALL_BLOCKS, *UPS, *DOWNS)
    for half, indices in enumerate((mask, vis)):
        sources[half] = table_rows(indices, table)

    def norms(rows):
        residual = queries[rows, :].astype(F32)
        source = residual + sources[0, rows, :]
        sources[0, rows, :] = source
        centred, _ = normalize(source)
        normed[0, rows, :] = (centred * row(e, 0) + row(e, 1)).astype(BF16)
        normed[3, rows, :] = (centred * row(e, 2) + row(e, 3)).astype(BF16)
        centred, _ = normalize(residual)
        normed[4, rows, :] = (centred * row(e, 4) + row(e, 5)).astype(BF16)
        incoming = latents[rows, :].astype(F32)
        source = incoming + sources[1, rows, :]
        sources[1, rows, :] = source
        centred, _ = normalize(source)
        normed[1, rows, :] = (centred * row(e, 2) + row(e, 3)).astype(BF16)
        centred, _ = normalize(incoming)
        normed[2, rows, :] = (centred * row(e, 4) + row(e, 5)).astype(BF16)

    each_rows(norms)
    copies.leave(normed, kept[0])
    copies.leave(sources, kept[5])
    weights.wait(0)
    qkvo = weights.held[0]
    flat[0] = ((dot(normed[0], qkvo[:, columns(0)]) + row(e, 6)).astype(BF16) * 0.125).astype(BF16)
    weights.wait(1)
    for m in (1, 3):
        flat[m] = dot(normed[m], qkvo[:, columns(1)]).astype(BF16)
    weights.wait(2)
    for m in (2, 4):
        flat[m] = (dot(normed[m], qkvo[:, columns(2)]) + row(e, 7)).astype(BF16)
    attention(copies, lens, which[0], 2, (flat, packed, probs, mixed, mixed_slots, regroup, ungroup), kept)
    weights.wait(3)
    summed = dot_nt(mixed[...], qkvo[:, columns(3)]) + row(e, 8)
    branch[...] = summed.astype(BF16)
    copies.leave(branch, kept[4])
    mid[...] = (queries[...].astype(F32) + row(e, 9) * summed).astype(BF16)
    feed_forward(copies, weights, mid, r, c, out, (f_normed, active, slope, f_branch), kept[6:])
    copies.finish()


def regressor_forward(lens, which, latents, queries, vis, mask, table, e, r, c, weights):
    made = pl.pallas_call(
        regressor_forward_kernel,
        in_specs=[SMEM, SMEM, *(VMEM for _ in range(8)), ANY],
        out_specs=(VMEM, VMEM, *(ANY for _ in STATE)),
        out_shape=(ROWS, ROWS, *STATE),
        scratch_shapes=state_scratch(2),
        compiler_params=params(56),
        name="regressor_forward",
    )(lens, which, latents, queries, vis, mask, table, e, r, c, weights)
    return made[0], made[1], tuple(made[2:])


def back_scratch(parts):
    rows = pltpu.VMEM((CAP, D), BF16)
    wide = pltpu.VMEM((CAP, FF), BF16)
    count = 1 + 2 * parts
    return [
        *WEIGHT_SCRATCH,
        wide,
        rows,
        wide,
        rows,
        pltpu.VMEM((count, PAD, D), BF16),
        pltpu.VMEM((IMGS, PAIRS, 2 * SLOT * parts, SLOT), BF16),
        rows,
        pltpu.VMEM((PAD, D), BF16),
        pltpu.VMEM((PAD, D), BF16),
        pltpu.VMEM((PAD, CAP), BF16),
        pltpu.VMEM((CAP, PAD), BF16),
        pltpu.VMEM((count, PAD, D), BF16),
        rows,
        pltpu.VMEM((2, CAP, D), F32),
        pltpu.VMEM((count, CAP, D), BF16),
        pltpu.VMEM((3 if parts == 2 else 1, CAP, D), F32),
        pltpu.VMEM((CAP, D), F32),
        pltpu.SemaphoreType.DMA((64,)),
    ]


def layer_back(parts, lens, pack, grads, mid, e, r, given, state, totals, kept, scratch):
    (
        *held, slope, f_branch, d_hidden, d_f_branch, packed, probs, branch, mixed_slots, d_slots, regroup, ungroup, d_packed,
        d_branch, sources, d_flat, work, residual, semaphores,
    ) = scratch
    copies = Copies(semaphores)
    weights = Weights(copies, given, held)
    parts_in = {"branch": copies.start(state[3], f_branch)}
    for i in ALL_BLOCKS:
        weights.start(2 * BLOCKS + i)
        parts_in[i] = copies.start(state[2].at[:, columns(i)], slope.at[:, columns(i)])
    weights.start(*UPS, 3)
    in_branch = copies.start(state[4], branch)
    in_packed = copies.start(state[0].at[pl.ds(0, 1 + 2 * parts)], packed)
    in_mixed = copies.start(state[6], mixed_slots)
    first = copies.take(IMGS)

    def probs_copy(j):
        source = state[1].at[j, :, pl.ds(0, 2 * SLOT * parts), :]
        return pltpu.make_async_copy(source, probs.at[j], semaphores.at[first + j])

    for j in range(IMGS):
        probs_copy(j).start()
    weights.start(0, 1, 2)
    in_sources = copies.start(state[5], sources) if parts == 2 else None
    totals[...] = jnp.zeros_like(totals)
    group_matrices(lens, pack, regroup, ungroup)
    feed_forward_back(
        copies, weights, lambda name: parts_in[name].wait(), grads, mid, r,
        (slope, f_branch, d_hidden, d_f_branch, work.at[0]), totals, kept[2:], residual,
    )
    in_branch.wait()
    last = 1 + 4 * parts

    def enter(rows, carry):
        g = residual[rows, :]
        low = (g * row(e, last)).astype(BF16)
        d_branch[rows, :] = low
        return carry[0] + colsum(low.astype(F32)), carry[1] + colsum(g * branch[rows, :].astype(F32))

    totals[last - 1 : last], totals[last : last + 1] = over_rows(enter, (zero_row(), zero_row()))
    copies.leave(d_branch, kept[1])
    weights.wait(3)
    d_mixed = dot(d_branch[...], weights.held[0][:, columns(3)]).astype(BF16)
    d_slots[...] = dot(regroup[...], d_mixed).astype(BF16)
    in_packed.wait()
    in_mixed.wait()
    attend_back(packed, probs, mixed_slots, d_slots, d_packed, parts, lambda j: probs_copy(j).wait())
    for m in range(1 + 2 * parts):
        d_flat[m] = dot(ungroup[...], d_packed[m]).astype(BF16)
        copies.leave(d_flat.at[m], kept[0].at[m])
    weights.wait(0, 1, 2)
    if in_sources is not None:
        in_sources.wait()
    return copies, weights.held[0]


def encoder_back_kernel(
    lens, which, g1, g2, x, mid, e, r, weights, s1, s2, s3, s4, s5, s6, s7, d_x, totals, k1, k2, k3, k4, *scratch
):
    *_, d_flat, work, residual, _ = scratch
    copies, qkvo = layer_back(
        1, lens, which[0], (g1, g2), mid, e, r, weights, (s1, s2, s3, s4, s5, s6, s7), totals, (k1, k2, k3, k4), scratch
    )
    d_normed = dot_nt(d_flat[0], qkvo[:, columns(0)])
    for m in (1, 2):
        d_normed += dot_nt(d_flat[m], qkvo[:, columns(m)])
    work[0] = d_normed

    def leave(rows, carry):
        grad = work[0, rows, :]
        normed, inverse = normalize(x[rows, :].astype(F32))
        d_x[rows, :] = (residual[rows, :] + norm_back(grad, row(e, 0), normed, inverse)).astype(BF16)
        terms = (grad * normed, grad, d_flat[0, rows, :].astype(F32), d_flat[2, rows, :].astype(F32))
        return tuple(total + colsum(term) for total, term in zip(carry, terms))

    sums = over_rows(leave, (zero_row(),) * 4)
    for i, total in enumerate(sums):
        totals[i : i + 1] = total
    copies.finish()


def back_state(state):
    return state[1], state[2], state[8], state[9], state[4], state[5], state[10]


def encoder_back(lens, which, g1, g2, x, mid, e, r, weights, state):
    made = pl.pallas_call(
        encoder_back_kernel,
        in_specs=[SMEM, SMEM, *(VMEM for _ in range(6)), *(ANY for _ in range(8))],
        out_specs=(VMEM, VMEM, *(ANY for _ in GRADS)),
        out_shape=(ROWS, TOTALS, *GRADS),
        scratch_shapes=back_scratch(1),
        compiler_params=params(56),
        name="encoder_back",
    )(lens, which, g1, g2, x, mid, e, r, weights, *back_state(state))
    return made[0], made[0], made[1], tuple(made[2:])


def regressor_back_kernel(
    lens, which, g, latents, queries, mid, e, r, weights, s1, s2, s3, s4, s5, s6, s7,
    d_latents, d_queries, totals, k1, k2, k3, k4, *scratch,
):
    *_, sources, d_flat, work, residual, _ = scratch
    copies, qkvo = layer_back(
        2, lens, which[0], (g,), mid, e, r, weights, (s1, s2, s3, s4, s5, s6, s7), totals, (k1, k2, k3, k4), scratch
    )

    def add(carry, terms):
        return tuple(total + colsum(term) for total, term in zip(carry, terms))

    for i, (m, block) in enumerate(((0, 0), (3, 1), (4, 2))):
        work[i] = dot_nt(d_flat[m], qkvo[:, columns(block)])

    def masked(rows, carry):
        normed, inverse = normalize(sources[0, rows, :])
        q_grad, k_grad, v_grad = (work[i, rows, :] for i in range(3))
        both = norm_back(q_grad, row(e, 0), normed, inverse) + norm_back(k_grad, row(e, 2), normed, inverse)
        v_normed, inverse = normalize(queries[rows, :].astype(F32))
        both += norm_back(v_grad, row(e, 4), v_normed, inverse)
        d_queries[rows, :] = (residual[rows, :] + both).astype(BF16)
        bias = d_flat[0, rows, :].astype(F32), d_flat[4, rows, :].astype(F32)
        return add(carry, (q_grad * normed, q_grad, k_grad * normed, k_grad, v_grad * v_normed, v_grad, *bias))

    sums = over_rows(masked, (zero_row(),) * 8)
    for i, (m, block) in enumerate(((1, 1), (2, 2))):
        work[i] = dot_nt(d_flat[m], qkvo[:, columns(block)])

    def visible(rows, carry):
        normed, inverse = normalize(sources[1, rows, :])
        k_grad, v_grad = (work[i, rows, :] for i in range(2))
        total = norm_back(k_grad, row(e, 2), normed, inverse)
        v_normed, inverse = normalize(latents[rows, :].astype(F32))
        d_latents[rows, :] = (total + norm_back(v_grad, row(e, 4), v_normed, inverse)).astype(BF16)
        bias = d_flat[2, rows, :].astype(F32)
        return add(carry, (k_grad * normed, k_grad, v_grad * v_normed, v_grad, bias))

    more = over_rows(visible, (*sums[2:6], sums[7]))
    for i, total in enumerate((*sums[:2], *more[:4], sums[6], more[4])):
        totals[i : i + 1] = total
    copies.finish()


def regressor_back(lens, which, g, latents, queries, mid, e, r, weights, state):
    made = pl.pallas_call(
        regressor_back_kernel,
        in_specs=[SMEM, SMEM, *(VMEM for _ in range(6)), *(ANY for _ in range(8))],
        out_specs=(VMEM, VMEM, VMEM, *(ANY for _ in GRADS)),
        out_shape=(ROWS, ROWS, TOTALS, *GRADS),
        scratch_shapes=back_scratch(2),
        compiler_params=params(56),
        name="regressor_back",
    )(lens, which, g, latents, queries, mid, e, r, weights, *back_state(state))
    return made[0], made[1], made[2], tuple(made[3:])


SHARE = BLOCKS + BLOCKS // 2


def weight_grads_kernel(parts, packs, *refs):
    step = pl.program_id(0)
    *base, out = refs[8 * packs :]
    inputs = [refs[8 * i : 8 * i + 8] for i in range(packs)]

    def put(terms):
        total = base[0][...].astype(F32) if base else None
        for term in terms:
            total = term if total is None else total + term
        out[...] = total.astype(BF16)

    @pl.when((step < 3) if parts == 1 else (step == 0))
    def _():
        put(dot_tn(n[0], p[step]) for n, p, *_ in inputs)

    if parts == 2:

        @pl.when((step == 1) | (step == 2))
        def _():
            put(dot_tn(n[step + more], p[step + more]) for n, p, *_ in inputs for more in (0, 2))

    @pl.when(step == 3)
    def _():
        put(dot_tn(b[...], m[...]) for _, _, m, b, *_ in inputs)

    @pl.when((step >= 4) & (step < 8))
    def _():
        put(dot_tn(n[...], h[...]) for *_, n, h, _, _ in inputs)

    @pl.when(step >= 8)
    def _():
        put(dot_tn(a[...], b[...]) for *_, a, b in inputs)


def grad_place(step):
    tail = jnp.maximum(step - 2 * BLOCKS, 0)
    late = jnp.where(step >= 2 * BLOCKS, 1, 0)
    section = (1 - late) * (step // BLOCKS) + late * (tail // 2)
    block = (1 - late) * (step % BLOCKS) + late * (BLOCKS + tail % 2)
    return section, block, 0, 0


def weight_grads(parts, states, grads, base=()):
    have = 1 if parts == 1 else 5
    made = 3 if parts == 1 else 5
    rows = full((CAP, D))
    up_part = pl.BlockSpec((CAP, D), lambda i: (0, jnp.clip(i - BLOCKS, 0, BLOCKS - 1)))
    down_part = pl.BlockSpec((CAP, D), lambda i: (0, jnp.clip(i - 2 * BLOCKS, 0, BLOCKS - 1)))
    placed = pl.BlockSpec((None, None, D, D), grad_place)
    one = [lead(have, (CAP, D)), lead(made, (CAP, D)), rows, rows, rows, up_part, down_part, rows]
    operands = []
    for s, g in zip(states, grads):
        operands += [s[0], g[0], s[3], g[1], s[6], g[2], s[7], g[3]]
    return pl.pallas_call(
        functools.partial(weight_grads_kernel, parts, len(states)),
        grid=(3 * BLOCKS,),
        in_specs=one * len(states) + [placed for _ in base],
        out_specs=placed,
        out_shape=sds((2, SHARE, D, D), BF16),
        compiler_params=params(),
        name="weight_grads",
    )(*operands, *base)


MESH = pl.DeviceIdType.MESH


def gather_weights_kernel(matrix, down, weights, send, receive, local):
    dp, section = lax.axis_index("dp"), lax.axis_index("section")
    odd = lax.rem(section, 2)
    partner = (dp, section + 1 - 2 * odd)
    barrier = pltpu.get_barrier_semaphore()
    pl.semaphore_signal(barrier, inc=1, device_id=partner, device_id_type=MESH)
    pl.semaphore_wait(barrier, 1)
    places = [(matrix.at[0, :, pl.ds(i * D, D)], odd * BLOCKS + i) for i in range(BLOCKS)]
    places += [(down.at[pl.ds(i * D, D), :], 2 * BLOCKS + odd * (BLOCKS // 2) + i) for i in range(BLOCKS // 2)]
    copies = []
    for i, (source, place) in enumerate(places):
        away = pltpu.make_async_remote_copy(
            source, weights.at[place], send.at[i], receive.at[i], device_id=partner, device_id_type=MESH
        )
        away.start()
        here = pltpu.make_async_copy(source, weights.at[place], local.at[i])
        here.start()
        copies += [away, here]
    for copy in copies:
        copy.wait()


def gather_weights(matrix, down):
    vmem = pl.BlockSpec(memory_space=pltpu.VMEM)
    return pl.pallas_call(
        gather_weights_kernel,
        in_specs=[vmem, vmem],
        out_specs=ANY,
        out_shape=sds((3 * BLOCKS, D, D), matrix.dtype),
        scratch_shapes=[pltpu.SemaphoreType.DMA((SHARE,)) for _ in range(3)],
        compiler_params=params(collective_id=1, has_side_effects=True),
        name="gather_weights",
    )(matrix, down)


RING = 8
SEGMENT = D // RING
PART = SEGMENT // 2
CHAIN = SHARE // 2


def ring_place(d):
    odd = lax.rem(d, 2)
    return (1 - odd) * lax.div(d, 2) + odd * (RING - 1 - lax.div(d, 2))


def ring_device(place):
    place = lax.rem(place + RING, RING)
    late = lax.div(place, RING // 2)
    return (1 - late) * 2 * place + late * (2 * (RING - 1 - place) + 1)


def reduce_kernel(
    grads, swapping, vectors, out_matrix, out_down, swapped, out_vectors,
    mine, partner_part, landing, final, stage, v_sum, v_in,
    pair_send, pair_receive, own_sem, ring_send, ring_receive, last_send, last_receive, out_sem,
    v_send, v_receive, swap_send, swap_receive,
):
    d, section = lax.axis_index("dp"), lax.axis_index("section")
    odd = lax.rem(section, 2)
    place = ring_place(d)
    across = (d, section + 2 - 4 * lax.div(section, 2))
    pair = (d, section + 1 - 2 * odd)
    ways = ((ring_device(place + 1), section), (ring_device(place - 1), section))

    def flipped(bit):
        return d + bit - 2 * bit * lax.rem(lax.div(d, bit), 2)

    levels = (pair, (flipped(1), section), (flipped(2), section), (flipped(4), section), across)
    barrier = pltpu.get_barrier_semaphore()
    for other in (*ways, *levels):
        pl.semaphore_signal(barrier, inc=1, device_id=other, device_id_type=MESH)
    pl.semaphore_wait(barrier, len(ways) + len(levels))

    def rows_of(step, way):
        segment = lax.rem(place + (step if way else -step) + 2 * RING, RING)
        return pl.ds(pl.multiple_of(segment * SEGMENT + way * PART, 8), PART)

    def remote(source, target, send, receive, device):
        return pltpu.make_async_remote_copy(source, target, send, receive, device_id=device, device_id_type=MESH)

    swap = remote(swapping, swapped, swap_send, swap_receive, across)
    swap.start()
    own = pltpu.make_async_copy(grads.at[odd], mine, own_sem)
    own.start()

    def pair_copy(step, way):
        rows = rows_of(step, way)
        return remote(
            grads.at[1 - odd, :, rows, :], partner_part.at[:, rows, :],
            pair_send.at[step, way], pair_receive.at[step, way], pair,
        )

    def start_pair(step, carry):
        for way in range(2):
            pair_copy(step, way).start()
        return carry

    lax.fori_loop(0, RING, start_pair, 0)

    def vector_copy(level):
        return remote(v_sum.at[level], v_in.at[level], v_send.at[level], v_receive.at[level], levels[level])

    def vector_next(level):
        vector_copy(level).wait()
        if level + 1 < len(levels):
            v_sum[level + 1] = v_sum[level] + v_in[level]
            vector_copy(level + 1).start()

    v_sum[0] = vectors[...]
    vector_copy(0).start()

    def blocks(chain):
        return pl.ds(chain * CHAIN, CHAIN)

    def ring_copy(step, way, chain):
        rows = rows_of(step, way)
        return remote(
            mine.at[blocks(chain), rows, :], landing.at[blocks(chain), rows, :],
            ring_send.at[step, way, chain], ring_receive.at[step, way, chain], ways[way],
        )

    def incoming(step, way, chain):
        rows = rows_of(step + 1, way)
        return remote(
            mine.at[blocks(chain), rows, :], landing.at[blocks(chain), rows, :],
            ring_send.at[step, way, chain], ring_receive.at[step, way, chain], ways[way],
        )

    own.wait()
    for way in range(2):
        pair_copy(0, way).wait_recv()
        rows = rows_of(0, way)
        for chain in range(2):
            part = (blocks(chain), rows, slice(None))
            mine[part] = (mine[part].astype(F32) + partner_part[part].astype(F32)).astype(BF16)
            ring_copy(0, way, chain).start()
    vector_next(0)

    def total_of(part):
        return (
            mine[part].astype(F32) + partner_part[part].astype(F32) + landing[part].astype(F32)
        ).astype(BF16)

    def reduce_step(step, carry):
        for chain in range(2):
            for way in range(2):
                if chain == 0:
                    pair_copy(step, way).wait_recv()
                incoming(step - 1, way, chain).wait_recv()
                part = (blocks(chain), rows_of(step, way), slice(None))
                mine[part] = total_of(part)
                ring_copy(step, way, chain).start()
        return carry

    lax.fori_loop(1, RING - 1, reduce_step, 0)
    vector_next(1)

    def last_copy(step, way, chain):
        rows = rows_of(step + RING - 1, way)
        return remote(
            final.at[blocks(chain), rows, :], final.at[blocks(chain), rows, :],
            last_send.at[step, way, chain], last_receive.at[step, way, chain], ways[way],
        )

    def last_incoming(step, way, chain):
        rows = rows_of(step + RING, way)
        return remote(
            final.at[blocks(chain), rows, :], final.at[blocks(chain), rows, :],
            last_send.at[step, way, chain], last_receive.at[step, way, chain], ways[way],
        )

    def out_copies(step, way, chain):
        rows = rows_of(step + RING - 1, way)
        copies = []
        for i in range(CHAIN):
            block = chain * CHAIN + i
            if block < BLOCKS:
                target = out_matrix.at[0, rows, pl.ds(block * D, D)]
            else:
                segment = lax.rem(place + (step + RING - 1 if way else 1 - step - RING) + 4 * RING, RING)
                start = (block - BLOCKS) * D + segment * SEGMENT + way * PART
                target = out_down.at[pl.ds(pl.multiple_of(start, 8), PART), :]
            copies.append(pltpu.make_async_copy(stage.at[way, chain, i], target, out_sem.at[way, chain, i]))
        return copies

    def write_out(step, way, chain, first):
        if not first:
            for copy in out_copies(step - 1, way, chain):
                copy.wait()
        stage[way, chain] = final[blocks(chain), rows_of(step + RING - 1, way), :].astype(F32)
        for copy in out_copies(step, way, chain):
            copy.start()

    for chain in range(2):
        for way in range(2):
            if chain == 0:
                pair_copy(RING - 1, way).wait_recv()
            incoming(RING - 2, way, chain).wait_recv()
            part = (blocks(chain), rows_of(RING - 1, way), slice(None))
            final[part] = total_of(part)
            last_copy(0, way, chain).start()
    vector_next(2)
    for chain in range(2):
        for way in range(2):
            write_out(0, way, chain, True)

    def gather_step(step, carry):
        for chain in range(2):
            for way in range(2):
                last_incoming(step - 1, way, chain).wait_recv()
                last_copy(step, way, chain).start()
                write_out(step, way, chain, False)
        return carry

    lax.fori_loop(1, 3, gather_step, 0)
    vector_next(3)
    lax.fori_loop(3, 5, gather_step, 0)
    vector_next(4)
    out_vectors[0] = v_sum[len(levels) - 1]
    out_vectors[1] = v_in[len(levels) - 1]
    lax.fori_loop(5, RING - 1, gather_step, 0)
    for chain in range(2):
        for way in range(2):
            last_incoming(RING - 2, way, chain).wait_recv()
            write_out(RING - 1, way, chain, False)
    for chain in range(2):
        for way in range(2):
            for copy in out_copies(RING - 1, way, chain):
                copy.wait()

    def all_sent(step, carry):
        for way in range(2):
            for chain in range(2):
                ring_copy(step, way, chain).wait_send()
                last_copy(step, way, chain).wait_send()
        return carry

    lax.fori_loop(0, RING - 1, all_sent, 0)

    def pair_sent(step, carry):
        for way in range(2):
            pair_copy(step, way).wait_send()
        return carry

    lax.fori_loop(0, RING, pair_sent, 0)
    swap.wait()


def reduce_grads(grads, swapping, vectors):
    share = (SHARE, D, D)
    vmem = pl.BlockSpec(memory_space=pltpu.VMEM)
    dma = pltpu.SemaphoreType.DMA
    return pl.pallas_call(
        reduce_kernel,
        in_specs=[ANY, ANY, vmem],
        out_specs=(ANY, ANY, ANY, vmem),
        out_shape=(
            sds((1, D, FF), F32),
            sds((FF // 2, D), F32),
            sds(swapping.shape, swapping.dtype),
            sds((2, VECTORS, D), F32),
        ),
        scratch_shapes=[
            pltpu.VMEM(share, BF16),
            pltpu.VMEM(share, BF16),
            pltpu.VMEM(share, BF16),
            pltpu.VMEM(share, BF16),
            pltpu.VMEM((2, 2, CHAIN, PART, D), F32),
            pltpu.VMEM((5, VECTORS, D), F32),
            pltpu.VMEM((5, VECTORS, D), F32),
            dma((RING, 2)),
            dma((RING, 2)),
            dma,
            dma((RING - 1, 2, 2)),
            dma((RING - 1, 2, 2)),
            dma((RING - 1, 2, 2)),
            dma((RING - 1, 2, 2)),
            dma((2, 2, CHAIN)),
            dma((5,)),
            dma((5,)),
            dma,
            dma,
        ],
        compiler_params=params(56, collective_id=2, has_side_effects=True),
        name="reduce_grads",
    )(grads, swapping, vectors)


def plain_reduce_grads(grads, swapping, vectors):
    odd = lax.rem(lax.axis_index("section"), 2)
    pair = [(0, 1), (1, 0), (2, 3), (3, 2)]
    theirs = lax.dynamic_index_in_dim(grads, 1 - odd, 0, keepdims=False)
    mine = lax.dynamic_index_in_dim(grads, odd, 0, keepdims=False)
    total = lax.psum(mine + lax.ppermute(theirs, "section", pair), "dp").astype(F32)
    vectors = lax.psum(vectors + lax.ppermute(vectors, "section", pair), "dp")
    matrix = jnp.swapaxes(total[:BLOCKS], 0, 1).reshape(1, D, FF)
    return (
        matrix,
        total[BLOCKS:].reshape(FF // 2, D),
        swap_layers(swapping),
        jnp.stack([vectors, swap_layers(vectors)]),
    )


def swap_layers(block):
    return lax.ppermute(block, "section", [(0, 2), (1, 3), (2, 0), (3, 1)])


def to_regressor(block):
    return lax.ppermute(block, "section", [(0, 2), (1, 3)])


def to_encoder(block):
    return lax.ppermute(block, "section", [(2, 0), (3, 1)])


def body(
    vis_embed, latent_cot, reg_queries, out_cot, section_matrix, down_weight, enc_vectors, reg_vectors,
    mlp_vectors, hidden_bias, pos_table, image_lengths, vis_index, mask_index,
):
    section = lax.axis_index("section")
    odd = lax.rem(section, 2)
    is_reg = section >= 2
    layer = jnp.where(is_reg, 1, 0)
    weights = gather_weights(section_matrix, down_weight)
    r = lax.dynamic_index_in_dim(mlp_vectors, layer, 0, keepdims=False)
    c = lax.dynamic_slice_in_dim(hidden_bias, layer, 1, 0)
    packs = [(odd + 2 * i).reshape(1).astype(jnp.int32) for i in range(2)]
    vis = [lax.dynamic_slice_in_dim(vis_index, (odd + 2 * i) * CAP, CAP)[:, None] for i in range(2)]
    mask = [lax.dynamic_slice_in_dim(mask_index, (odd + 2 * i) * CAP, CAP)[:, None] for i in range(2)]

    incoming = swap_layers(jnp.where(is_reg, vis_embed, reg_queries))
    x = [vis_embed, incoming]
    queries = [incoming, reg_queries]

    def enc_forward(i):
        return encoder_forward(image_lengths, packs[i], x[i], enc_vectors, r, c, weights)

    def reg_forward(i, latents):
        return regressor_forward(
            image_lengths, packs[i], latents, queries[i], vis[i], mask[i], pos_table, reg_vectors, r, c, weights
        )

    def no_forward():
        made = unset((ROWS, ROWS, *STATE))
        return made[0], made[1], tuple(made[2:])

    def enc_back(i, d_latents, kept):
        return encoder_back(
            image_lengths, packs[i], lat_cot[i], d_latents, x[i], kept[0], enc_vectors, r, weights, kept[2]
        )

    def reg_back(i, latents, kept):
        return regressor_back(
            image_lengths, packs[i], cot[i], latents, queries[i], kept[0], reg_vectors, r, weights, kept[2]
        )

    def no_back():
        made = unset((ROWS, ROWS, TOTALS, *GRADS))
        return made[0], made[1], made[2], tuple(made[3:])

    def on_encoder(work, otherwise):
        return lax.cond(is_reg, otherwise, work)

    def on_regressor(work, otherwise):
        return lax.cond(is_reg, work, otherwise)

    enc1 = on_encoder(lambda: enc_forward(0), no_forward)
    latents1 = to_regressor(enc1[1])
    swapped_cot = swap_layers(jnp.where(is_reg, latent_cot, out_cot))
    lat_cot = [latent_cot, swapped_cot]
    cot = [swapped_cot, out_cot]
    enc2 = on_encoder(lambda: enc_forward(1), no_forward)
    latents2 = to_regressor(enc2[1])

    def reg_first():
        state = reg_forward(0, latents1)
        return state, reg_back(0, latents1, state)

    reg1, reg_grads1 = on_regressor(reg_first, lambda: (no_forward(), no_back()))
    d_latents1 = to_encoder(reg_grads1[0])
    reg2 = on_regressor(lambda: reg_forward(1, latents2), no_forward)
    reg_grads2 = on_regressor(lambda: reg_back(1, latents2, reg2), no_back)
    d_latents2 = to_encoder(reg_grads2[0])
    share = sds((2, SHARE, D, D), BF16)

    def enc_back1():
        grads = enc_back(0, d_latents1, enc1)
        return grads, weight_grads(1, (enc1[2],), (grads[3],))

    enc_grads1, enc_share = on_encoder(enc_back1, lambda: (no_back(), unset((share,))[0]))

    def reg_last():
        return (
            weight_grads(2, (reg1[2], reg2[2]), (reg_grads1[3], reg_grads2[3])),
            reg_grads1[2] + reg_grads2[2],
            jnp.stack([reg1[1], reg_grads1[1]]),
        )

    def enc_last():
        grads = enc_back(1, d_latents2, enc2)
        return (
            weight_grads(1, (enc2[2],), (grads[3],), (enc_share,)),
            enc_grads1[2] + grads[2],
            jnp.stack([grads[0], grads[0]]),
        )

    grads, vectors, swapping = lax.cond(is_reg, reg_last, enc_last)
    reduce = reduce_grads if lax.axis_size("dp") == RING else plain_reduce_grads
    matrix_grad, down_grad, swapped, vectors = reduce(grads, swapping, vectors)

    def pick(reg, enc):
        return jnp.where(is_reg, reg, enc)

    latents = pick(latents2, enc1[1])
    regressed = pick(reg2[1], swapped[0])
    vis_grad = pick(swapped[0], enc_grads1[0])
    query_grad = pick(reg_grads2[1], swapped[1])
    enc_total, reg_total = pick(vectors[1], vectors[0]), pick(vectors[0], vectors[1])
    return (
        latents,
        regressed,
        vis_grad,
        query_grad,
        matrix_grad,
        down_grad,
        enc_total[:6],
        reg_total[:10],
        jnp.stack([enc_total[FFN_AT:HIDDEN_AT], reg_total[FFN_AT:HIDDEN_AT]]),
        jnp.stack([t[HIDDEN_AT : HIDDEN_AT + BLOCKS].reshape(FF) for t in (enc_total, reg_total)]),
    )


def solution(mesh):
    rows = P(("dp", "section"), None)
    in_specs = (
        rows, rows, rows, rows, P("section", None, None), P("section", None),
        P(), P(), P(), P(), P(), P("dp", None), P("dp"), P("dp"),
    )
    out_specs = (rows, rows, rows, rows, P("section", None, None), P("section", None), P(), P(), P(), P())
    return jax.shard_map(body, mesh=mesh, in_specs=in_specs, out_specs=out_specs, check_vma=False)
```

time: 476 us -> 427 us (0.90)
  waiting for transfers between devices: 101 us -> 58.7 us
  starting transfers between devices: 29.4 us -> 8.31 us
  loops' own time: 17.9 us -> 26.6 us
  Pallas kernels: 289 us -> 295 us
    ppermute x2, waiting for transfers between devices: 21.8 us -> 0.01 us  [to_regressor(): return lax.ppermute(block, 'section', [(0, 2), (1, 3)])]
    ppermute x2, starting transfers between devices: 23.9 us -> 2.65 us  [to_regressor(): return lax.ppermute(block, 'section', [(0, 2), (1, 3)])]
    ppermute x2, waiting for transfers between devices: 79.7 us -> 58.7 us  [to_encoder(): return lax.ppermute(block, 'section', [(2, 0), (3, 1)])]
    another operation x6 -> x7, loops' own time: 17.9 us -> 26.6 us  [the longest x3 25.3 us: on_regressor(): return lax.cond(is_reg, work, otherwise)]
    pallas_call x10 -> x7, Pallas kernels: 142 us -> 147 us  [the longest x2 53 us: encoder_back(): pl.pallas_call(encoder_back_kernel, in_specs=[SMEM, SMEM, *(VMEM for _ in...]
    unnamed x41 -> x39, local copies, waits for them, and re-layouts: 11.8 us -> 11 us
  transfers between devices with their start and end apart: 5 -> 6, of which waited for: 4 -> 2; matrix products, arithmetic and copies ran while one was open for 1% -> 1% of each run, Pallas kernels for 8% -> 24%
where the time goes in v2:
time: 427 us; the launch traced here: 422 us
  Pallas kernels  295 us (69%)
  waiting for transfers between devices  58.7 us (14%)
  loops' own time  26.6 us (6%)
  local copies, waits for them, and re-layouts  19.8 us (5%)
  other arithmetic  11.8 us (3%)
  starting transfers between devices  8.31 us (2%)
    pallas_call x1, Pallas kernels, reduce_grads(): pl.pallas_call(reduce_kernel, in_specs=[ANY, ANY, vmem], out_specs=(ANY,...  148 us
    ppermute x2, waiting for transfers between devices, to_encoder(): return lax.ppermute(block, 'section', [(2, 0), (3, 1)])  58.7 us
    pallas_call x2, Pallas kernels, encoder_back(): pl.pallas_call(encoder_back_kernel, in_specs=[SMEM, SMEM, *(VMEM for _ in...  53 us
    pallas_call x2, Pallas kernels, encoder_forward(): pl.pallas_call(encoder_forward_kernel, in_specs=[SMEM, SMEM, VMEM, VMEM,...  47.4 us
    pallas_call x2, Pallas kernels, weight_grads(): pl.pallas_call(functools.partial(weight_grads_kernel, parts, len(states))...  32.8 us
    another operation x3, loops' own time, on_regressor(): return lax.cond(is_reg, work, otherwise)  25.3 us
    pallas_call x1, Pallas kernels, gather_weights(): pl.pallas_call(gather_weights_kernel, in_specs=[vmem, vmem], out_specs=AN...  14 us
    unnamed x39, local copies, waits for them, and re-layouts  11 us
  transfers between devices with their start and end apart: 6, of which 2 were waited for; matrix products, arithmetic and copies ran while one was open for 1% of the time, Pallas kernels for 24%

profile of v2, /device:TPU:0, one launch (start us, length us, event | category | flops | bytes accessed | tf_op | source)
XLA Modules:
  0.0 421.9 jit_solution(9744205617998338883)
XLA Ops:
  0.7 2.1 broadcast_select_fusion.2
  2.8 2.9 collective-permute-start
  5.7 2.0 broadcast_select_fusion
  7.7 14.0 %gather_weights.1 = bf16[12,768,768]{2,1,0:T(8,128)(2,1)} custom-call(bf16[1,768,3072]{2,1,0:T(8,128)(2,1)} %matrix.1, bf16[1536,768]{1,0:T(8,128)(2,1)S(1)} %copy-done.4), custom_call_target="tpu_custom_call" | custom-call | tf_op jit(solution)/shard_map/gather_weights/pallas_call | solution.py:806
  21.8 23.8 %conditional.8 = ((bf16[384,768]{1,0:T(8,128)(2,1)}, bf16[384,768]{1,0:T(8,128)(2,1)S(1)}, bf16[5,384,768]{2,1,0:T(8,128)(2,1)}, bf16[5,512,768]{2,1,0:T(8,128)(...) conditional(s32[]{:T(128)} %convert_element_type.2, ...), branch_computations={%region_2.3_spmd, %region_3.4_spmd} | conditional | bytes 8 | solution.py:1145
  21.8 23.4 %encoder_forward.3 = (bf16[384,768]{1,0:T(8,128)(2,1)}, bf16[384,768]{1,0:T(8,128)(2,1)S(1)}, bf16[5,384,768]{2,1,0:T(8,128)(2,1)}, bf16[5,512,768]{2,1,0:T(8,12...) custom-call(s32[4,4]{1,0:T(4,128)S(1)} %get-tuple-element.241.lens, ...), custom_call_target="tpu_custom_call" | custom-call | tf_op jit(solution)/shard_map/cond/branch_0_fun/encoder_forward/pallas_call | solution.py:442
  47.0 24.1 %conditional.7 = ((bf16[384,768]{1,0:T(8,128)(2,1)}, bf16[384,768]{1,0:T(8,128)(2,1)}, bf16[5,384,768]{2,1,0:T(8,128)(2,1)}, bf16[5,512,768]{2,1,0:T(8,128)(2,1)...) conditional(s32[]{:T(128)} %convert_element_type.2, ...), branch_computations={%region_0.1_spmd, %region_1.2_spmd} | conditional | bytes 8 | solution.py:1145
  47.0 23.9 %encoder_forward.2 = (bf16[384,768]{1,0:T(8,128)(2,1)}, bf16[384,768]{1,0:T(8,128)(2,1)}, bf16[5,384,768]{2,1,0:T(8,128)(2,1)}, bf16[5,512,768]{2,1,0:T(8,128)(2...) custom-call(s32[4,4]{1,0:T(4,128)S(1)} %get-tuple-element.234.lens, ...), custom_call_target="tpu_custom_call" | custom-call | tf_op jit(solution)/shard_map/cond/branch_0_fun/encoder_forward/pallas_call | solution.py:442
  72.6 12.7 %conditional.11 = (bf16[384,768]{1,0:T(8,128)(2,1)}, bf16[5,384,768]{2,1,0:T(8,128)(2,1)}, bf16[384,768]{1,0:T(8,128)(2,1)}, bf16[384,768]{1,0:T(8,128)(2,1)}, b...) conditional(s32[]{:T(128)} %convert_element_type.2, () %tuple.67, ...), branch_computations={%region_8.9_spmd, %region_9.10_spmd.clone} | conditional | bytes 12392 | solution.py:1148
  86.6 12.6 %conditional.9 = ((bf16[384,768]{1,0:T(8,128)(2,1)}, bf16[384,768]{1,0:T(8,128)(2,1)}, bf16[5,384,768]{2,1,0:T(8,128)(2,1)}, bf16[5,512,768]{2,1,0:T(8,128)(2,1)...) conditional(s32[]{:T(128)} %convert_element_type.2, () %tuple.63, ...), branch_computations={%region_4.5_spmd, %region_5.6_spmd.clone} | conditional | bytes 12304 | solution.py:1148
  100.7 40.4 %collective-permute-done.5 = bf16[384,768]{1,0:T(8,128)(2,1)} collective-permute-done((bf16[384,768]{1,0:T(8,128)(2,1)}, bf16[384,768]{1,0:T(8,128)(2,1)}, u32[]{:S(2)}, u32[]{:S(2)}) %collective-permute-start.5) | collective-permute-done | bytes 589856 | tf_op jit(solution)/shard_map/ppermute | solution.py:1096
  141.1 45.4 %conditional.12 = (bf16[384,768]{1,0:T(8,128)(2,1)}, f32[24,768]{1,0:T(8,128)S(1)}, bf16[2,6,768,768]{3,2,1,0:T(8,128)(2,1)}) conditional(s32[]{:T(128)} %convert_element_type.2, (s32[4,4]{1,0:T(4,128)S(1)}, s32[1]{0:T(128)}, bf16[384,768]{1,0:T(8,128)(2,1)}, bf16[384,768]{1,0:T(8,128)(2,1)}, bf16[384,768]{1,0:T(8,128)(2,1)S(1)}, ...), branch_computations={%region_10.11_spmd, %region_11.12_spmd} | conditional | bytes 30671040 | solution.py:1145
  141.1 26.2 %encoder_back.2 = (bf16[384,768]{1,0:T(8,128)(2,1)}, f32[24,768]{1,0:T(8,128)S(1)}, bf16[5,384,768]{2,1,0:T(8,128)(2,1)}, bf16[384,768]{1,0:T(8,128)(2,1)}, bf16...) custom-call(s32[4,4]{1,0:T(4,128)S(1)} %get-tuple-element.319.lens, s32[1]{0:T(128)} %get-tuple-element.320.which, ...), custom_call_target="tpu_custom_call" | custom-call | tf_op jit(solution)/shard_map/cond/branch_0_fun/encoder_back/pallas_call | solution.py:643
  167.4 1.7 copy-done.3
  171.2 15.0 %weight_grads.3 = bf16[2,6,768,768]{3,2,1,0:T(8,128)(2,1)} custom-call(bf16[5,384,768]{2,1,0:T(8,128)(2,1)S(1)} %copy-done.13, bf16[5,384,768]{2,1,0:T(8,128)(2,1)} %get-tuple-element.338.refs_1_, bf16[384,768]{1,0:T(8,128)(2,1)S(1)} %copy-done.18, bf16[384,768]{1,0:T(8,128)(2,1)S(1)} %copy-done.5, bf16[384,768]{1,0:T(8,128)(2,1)S(1)} %copy-done.19, ...), custom_call_target="tpu_custom_call" | custom-call | tf_op jit(solution)/shard_map/cond/branch_0_fun/weight_grads/pallas_call | solution.py:768
  186.5 2.0 broadcast_select_fusion.1
  188.5 18.3 %collective-permute-done.3 = bf16[384,768]{1,0:T(8,128)(2,1)} collective-permute-done((bf16[384,768]{1,0:T(8,128)(2,1)}, bf16[384,768]{1,0:T(8,128)(2,1)}, u32[]{:S(2)}, u32[]{:S(2)}) %collective-permute-start.3) | collective-permute-done | bytes 589856 | tf_op jit(solution)/shard_map/ppermute | solution.py:1096
  206.8 48.8 %conditional.13 = (bf16[2,6,768,768]{3,2,1,0:T(8,128)(2,1)}, bf16[2,384,768]{2,1,0:T(8,128)(2,1)S(1)}, f32[24,768]{1,0:T(8,128)S(1)}, f32[24,768]{1,0:T(8,128)S(1)}) conditional(s32[]{:T(128)} %convert_element_type.2, (s32[4,4]{1,0:T(4,128)S(1)}, s32[1]{0:T(128)}, bf16[384,768]{1,0:T(8,128)(2,1)}, bf16[384,768]{1,0:T(8,128)(2,1)}, ...), branch_computations={%region_12.13_spmd, %region_13.14_spmd} | conditional | flops 589824 | bytes 44237056 | solution.py:1190
  206.8 26.8 %encoder_back.3 = (bf16[384,768]{1,0:T(8,128)(2,1)}, f32[24,768]{1,0:T(8,128)S(1)}, bf16[5,384,768]{2,1,0:T(8,128)(2,1)}, bf16[384,768]{1,0:T(8,128)(2,1)}, bf16...) custom-call(s32[4,4]{1,0:T(4,128)S(1)} %get-tuple-element.348.lens, s32[1]{0:T(128)} %get-tuple-element.349.which, ...), custom_call_target="tpu_custom_call" | custom-call | tf_op jit(solution)/shard_map/cond/branch_0_fun/encoder_back/pallas_call | solution.py:643
  237.5 17.9 %weight_grads.4 = bf16[2,6,768,768]{3,2,1,0:T(8,128)(2,1)} custom-call(bf16[5,384,768]{2,1,0:T(8,128)(2,1)S(1)} %copy-done.14, bf16[5,384,768]{2,1,0:T(8,128)(2,1)} %get-tuple-element.364.refs_1_, bf16[384,768]{1,0:T(8,128)(2,1)S(1)} %copy-done.22, bf16[384,768]{1,0:T(8,128)(2,1)S(1)} %copy-done.7, bf16[384,768]{1,0:T(8,128)(2,1)S(1)} %copy-done.23, ...), custom_call_target="tpu_custom_call" | custom-call | tf_op jit(solution)/shard_map/cond/branch_0_fun/weight_grads/pallas_call | solution.py:768
  256.3 148.2 %reduce_grads.1 = (f32[1,768,3072]{2,1,0:T(8,128)}, f32[1536,768]{1,0:T(8,128)}, bf16[2,384,768]{2,1,0:T(8,128)(2,1)}, f32[2,24,768]{2,1,0:T(8,128)}) custom-call(bf16[2,6,768,768]{3,2,1,0:T(8,128)(2,1)} %get-tuple-element.533.grads, bf16[2,384,768]{2,1,0:T(8,128)(2,1)S(1)} %get-tuple-element.534.swapping, f32[24,768]{1,0:T(8,128)} %add.24.vectors), custom_call_target="tpu_custom_call" | custom-call | tf_op jit(solution)/shard_map/reduce_grads/pallas_call | solution.py:1035
  408.0 2.8 bitcast_select_fusion
  410.8 8.7 %copy.162 = f32[1,768,3072]{2,1,0:T(8,128)} copy(f32[1,768,3072]{2,1,0:T(8,128)} %get-tuple-element.782) | data formatting | bytes 18874368
  419.5 2.2 copy.163
  (88 shorter events, 15.7 us)
Async XLA Ops:
  2.8 44.2 %collective-permute-start = (bf16[384,768]{1,0:T(8,128)(2,1)}, bf16[384,768]{1,0:T(8,128)(2,1)S(1)}, u32[]{:S(2)}, u32[]{:S(2)}) collective-permute-start(bf16[384,768]{1,0:T(8,128)(2,1)} %broadcast_select_fusion.2), channel_id=1, source_target_pairs={{0,2},{1,3},{2,0},{3,1},{4,6},{5,7},{6,4},{7,5},{8,10},{9,11},{10,... | collective-permute-start | bytes 1769480 | tf_op jit(solution)/shard_map/ppermute | solution.py:1088
  7.7 64.8 %collective-permute-start.2 = (bf16[384,768]{1,0:T(8,128)(2,1)}, bf16[384,768]{1,0:T(8,128)(2,1)}, u32[]{:S(2)}, u32[]{:S(2)}) collective-permute-start(bf16[384,768]{1,0:T(8,128)(2,1)} %broadcast_select_fusion), channel_id=1, source_target_pairs={{0,2},{1,3},{2,0},{3,1},{4,6},{5,7},{6,4},{7,5},{8,10},{9,11},{10,... | collective-permute-start | bytes 1769480 | tf_op jit(solution)/shard_map/ppermute | solution.py:1088
  7.7 14.0 %copy-start.26 = (f32[2,3072]{1,0:T(2,128)S(1)}, f32[2,3072]{1,0:T(2,128)}, u32[]{:S(2)}) copy-start(f32[2,3072]{1,0:T(2,128)} %param.37) | copy-start | bytes 73732
  7.7 14.1 %copy-start.10 = (bf16[384,768]{1,0:T(8,128)(2,1)S(1)}, bf16[384,768]{1,0:T(8,128)(2,1)}, u32[]{:S(2)}) copy-start(bf16[384,768]{1,0:T(8,128)(2,1)} %param.28) | copy-start | bytes 1769476
  7.7 14.1 %copy-start.24 = (f32[6,768]{1,0:T(8,128)S(1)}, f32[6,768]{1,0:T(8,128)}, u32[]{:S(2)}) copy-start(f32[6,768]{1,0:T(8,128)} %param.34) | copy-start | bytes 55300
  7.7 14.0 %copy-start.25 = (s32[4,4]{1,0:T(4,128)S(1)}, s32[4,4]{1,0:T(4,128)}, u32[]{:S(2)}) copy-start(s32[4,4]{1,0:T(4,128)} %param.39) | copy-start | bytes 196
  45.6 26.9 %collective-permute-start.4 = (bf16[384,768]{1,0:T(8,128)(2,1)S(1)}, bf16[384,768]{1,0:T(8,128)(2,1)S(1)}, u32[]{:S(2)}, u32[]{:S(2)}) collective-permute-start(bf16[384,768]{1,0:T(8,128)(2,1)S(1)} %get-tuple-element.475), channel_id=1, source_target_pairs={{0,2},{1,3},{4,6},{5,7},{8,10},{9,11},{12,14},{13,15},{16,18},{17,... | collective-permute-start | bytes 1769480 | tf_op jit(solution)/shard_map/ppermute | solution.py:1092
  47.0 25.6 %copy-start.12 = (f32[256,768]{1,0:T(8,128)S(1)}, f32[256,768]{1,0:T(8,128)}, u32[]{:S(2)}) copy-start(f32[256,768]{1,0:T(8,128)} %param.38) | copy-start | bytes 2359300
  47.0 25.6 %copy-start.17 = (f32[10,768]{1,0:T(8,128)S(1)}, f32[10,768]{1,0:T(8,128)}, u32[]{:S(2)}) copy-start(f32[10,768]{1,0:T(8,128)} %param.35) | copy-start | bytes 92164
  47.0 25.6 %copy-start.27 = (s32[1536]{0:T(1024)S(1)}, s32[1536]{0:T(1024)}, u32[]{:S(2)}) copy-start(s32[1536]{0:T(1024)} %param.40) | copy-start | bytes 18436
  47.0 25.5 %copy-start.28 = (s32[1536]{0:T(1024)S(1)}, s32[1536]{0:T(1024)}, u32[]{:S(2)}) copy-start(s32[1536]{0:T(1024)} %param.41) | copy-start | bytes 18436
  71.1 15.4 %collective-permute-start.1 = (bf16[384,768]{1,0:T(8,128)(2,1)}, bf16[384,768]{1,0:T(8,128)(2,1)S(1)}, u32[]{:S(2)}, u32[]{:S(2)}) collective-permute-start(bf16[384,768]{1,0:T(8,128)(2,1)} %get-tuple-element.474), channel_id=1, source_target_pairs={{0,2},{1,3},{4,6},{5,7},{8,10},{9,11},{12,14},{13,15},{16,18},{17,... | collective-permute-start | bytes 1769480 | tf_op jit(solution)/shard_map/ppermute | solution.py:1092
  72.5 14.0 %copy-start.9 = (bf16[384,768]{1,0:T(8,128)(2,1)S(1)}, bf16[384,768]{1,0:T(8,128)(2,1)}, u32[]{:S(2)}) copy-start(bf16[384,768]{1,0:T(8,128)(2,1)} %param.30) | copy-start | bytes 1769476
  85.3 55.9 %collective-permute-start.5 = (bf16[384,768]{1,0:T(8,128)(2,1)}, bf16[384,768]{1,0:T(8,128)(2,1)}, u32[]{:S(2)}, u32[]{:S(2)}) collective-permute-start(bf16[384,768]{1,0:T(8,128)(2,1)} %get-tuple-element.498), channel_id=1, source_target_pairs={{2,0},{3,1},{6,4},{7,5},{10,8},{11,9},{14,12},{15,13},{18,16},{19,... | collective-permute-start | bytes 1769480 | tf_op jit(solution)/shard_map/ppermute | solution.py:1096
  99.3 41.9 %copy-start.11 = (bf16[384,768]{1,0:T(8,128)(2,1)S(1)}, bf16[384,768]{1,0:T(8,128)(2,1)}, u32[]{:S(2)}) copy-start(bf16[384,768]{1,0:T(8,128)(2,1)} %param.28) | copy-start | bytes 1769476
  99.3 107.5 %collective-permute-start.3 = (bf16[384,768]{1,0:T(8,128)(2,1)}, bf16[384,768]{1,0:T(8,128)(2,1)}, u32[]{:S(2)}, u32[]{:S(2)}) collective-permute-start(bf16[384,768]{1,0:T(8,128)(2,1)} %get-tuple-element.485), channel_id=1, source_target_pairs={{2,0},{3,1},{6,4},{7,5},{10,8},{11,9},{14,12},{15,13},{18,16},{19,... | collective-permute-start | bytes 1769480 | tf_op jit(solution)/shard_map/ppermute | solution.py:1096
  141.1 26.2 %copy-start.13 = (bf16[5,384,768]{2,1,0:T(8,128)(2,1)S(1)}, bf16[5,384,768]{2,1,0:T(8,128)(2,1)}, u32[]{:S(2)}) copy-start(bf16[5,384,768]{2,1,0:T(8,128)(2,1)} %get-tuple-element.337.refs_0_) | copy-start | bytes 8847364 | tf_op jit(solution)/shard_map/cond
  141.1 26.2 %copy-start.18 = (bf16[384,768]{1,0:T(8,128)(2,1)S(1)}, bf16[384,768]{1,0:T(8,128)(2,1)}, u32[]{:S(2)}) copy-start(bf16[384,768]{1,0:T(8,128)(2,1)} %get-tuple-element.339.refs_2_) | copy-start | bytes 1769476 | tf_op jit(solution)/shard_map/cond
  141.1 26.2 %copy-start.19 = (bf16[384,768]{1,0:T(8,128)(2,1)S(1)}, bf16[384,768]{1,0:T(8,128)(2,1)}, u32[]{:S(2)}) copy-start(bf16[384,768]{1,0:T(8,128)(2,1)} %get-tuple-element.341.refs_4_) | copy-start | bytes 1769476 | tf_op jit(solution)/shard_map/cond
  206.8 26.8 %copy-start.14 = (bf16[5,384,768]{2,1,0:T(8,128)(2,1)S(1)}, bf16[5,384,768]{2,1,0:T(8,128)(2,1)}, u32[]{:S(2)}) copy-start(bf16[5,384,768]{2,1,0:T(8,128)(2,1)} %get-tuple-element.347.refs_0_) | copy-start | bytes 8847364 | tf_op jit(solution)/shard_map/cond
  206.8 26.8 %copy-start.15 = (bf16[384,3072]{1,0:T(8,128)(2,1)S(1)}, bf16[384,3072]{1,0:T(8,128)(2,1)}, u32[]{:S(2)}) copy-start(bf16[384,3072]{1,0:T(8,128)(2,1)} %get-tuple-element.369.refs_6_) | copy-start | bytes 7077892 | tf_op jit(solution)/shard_map/cond
  206.8 26.8 %copy-start.22 = (bf16[384,768]{1,0:T(8,128)(2,1)S(1)}, bf16[384,768]{1,0:T(8,128)(2,1)}, u32[]{:S(2)}) copy-start(bf16[384,768]{1,0:T(8,128)(2,1)} %get-tuple-element.365.refs_2_) | copy-start | bytes 1769476 | tf_op jit(solution)/shard_map/cond
  206.8 26.8 %copy-start.23 = (bf16[384,768]{1,0:T(8,128)(2,1)S(1)}, bf16[384,768]{1,0:T(8,128)(2,1)}, u32[]{:S(2)}) copy-start(bf16[384,768]{1,0:T(8,128)(2,1)} %get-tuple-element.367.refs_4_) | copy-start | bytes 1769476 | tf_op jit(solution)/shard_map/cond
  237.5 17.9 %copy-start.20 = (bf16[384,768]{1,0:T(8,128)(2,1)S(1)}, bf16[384,768]{1,0:T(8,128)(2,1)}, u32[]{:S(2)}) copy-start(bf16[384,768]{1,0:T(8,128)(2,1)} %get-tuple-element.372) | copy-start | bytes 1769476 | tf_op jit(solution)/shard_map/cond
  (13 other events, 66.7 us)
